TPU v7x, 256 devices: a whole 4x4x8 slice. The times are simulated.
256 devices in a mesh: member: 8 (over x_hi, y), lat: 16 (over z, core), lon: 2 (over x_lo).
Axes of the slice: x: 4 (x_hi: 2, x_lo: 2; x = x_hi * 2 + x_lo), y: 4, z: 8, core: 2. Of those that a mesh axis runs over, the one named last changes fastest.
Arguments:
- state: bfloat16 [72, 128, 256], P(None, 'lat', 'lon'), may hold values from -6 to 6
- noise: bfloat16 [8, 2, 8, 128, 256], P('member', None, None, 'lat', 'lon'), may hold values from -6 to 6
- target: bfloat16 [2, 72, 128, 256], P(None, None, 'lat', 'lon'), may hold values from -6 to 6
- encoder_state_weight: bfloat16 [512, 72], replicated, may hold values from -0.75 to 0.75
- enc_noise: bfloat16 [512, 8], replicated, may hold values from -2 to 2
- lat_taps: float32 [4, 7, 512], replicated, may hold values from -1.75 to 1.75
- lon_taps: float32 [4, 6, 512], replicated, may hold values from -1.75 to 1.75
- gains: float32 [4, 512], replicated, may hold values from 0.25 to 1.75
- mix: bfloat16 [4, 512, 512], replicated, may hold values from -0.25 to 0.25
- decode: bfloat16 [72, 512], replicated, may hold values from -0.25 to 0.25
Outputs:
- trajectory_predictions: bfloat16 [8, 2, 72, 128, 256], P('member', None, None, 'lat', 'lon')
- probabilistic_error: float32 [72, 128, 256], P('member', 'lat', 'lon')
All inputs are finite; a program needn't handle non-finite values.
Results may differ from a plain program's by a relative error of at most 0.015.
Values may be sent and summed in bfloat16 or wider, within the bound.
No kernel may reach another device: no remote copies, remote signals or barrier semaphores. Data moves between devices by JAX's collectives and lax.ppermute only.
A program may use at most 64 MiB of HBM per device.

v0:
```python
import functools

import jax
import jax.numpy as jnp
from jax import lax
from jax.experimental import pallas as pl
from jax.experimental.pallas import tpu as pltpu
from jax.sharding import PartitionSpec as P

epsilon = 1e-05
REACH = 3
F32 = jnp.float32
BF16 = jnp.bfloat16


def step_kernel(
    layers,
    variables,
    carry_noise,
    up_ref,
    own_ref,
    down_ref,
    enc_ref,
    taps_ref,
    mix_ref,
    dec_ref,
    out_ref,
    h_ref,
    v_ref,
    acc_ref,
):
    halo = up_ref.shape[0]
    own = own_ref.shape[0]
    channels = h_ref.shape[1]
    lanes = h_ref.shape[2]
    inputs = enc_ref.shape[1]
    group = 16
    blocks = channels // group
    band = lax.axis_index("lat") // 2
    first = band * own - halo
    height = (lax.axis_size("lat") // 2) * own

    enc = enc_ref[...]

    def encode(source, offset):
        def pair(k, _):
            x = jnp.concatenate([source[2 * k, :inputs], source[2 * k + 1, :inputs]], axis=1)
            y = jnp.dot(enc, x, preferred_element_type=F32).astype(BF16)
            h_ref[offset + 2 * k] = y[:, :lanes]
            h_ref[offset + 2 * k + 1] = y[:, lanes:]
            return 0

        lax.fori_loop(0, source.shape[0] // 2, pair, 0)

    encode(up_ref, 0)
    encode(own_ref, halo)
    encode(down_ref, halo + own)

    c0 = 2.0 * 0.7978845608028654
    c1 = 8.0 * 0.7978845608028654 * 0.044715

    def layer(level, _):
        out_rows = own + 2 * halo - 2 * REACH * (level + 1)

        def pair(k, _):
            k = 2 * k
            sums = [jnp.zeros((group, lanes), F32) for _ in range(4)]
            for part in range(blocks // 4):
                small = [None] * 4
                for sub in range(4):
                    b = part * 4 + sub
                    span = pl.ds(b * group, group)
                    rows = [h_ref[k + i, span, :] for i in range(8)]
                    for r in range(2):
                        mid = rows[r + REACH]
                        total = None
                        for d in range(7):
                            term = taps_ref[level, d, span, :] * rows[r + d]
                            total = term if total is None else total + term
                        for column, d in enumerate([-3, -2, -1, 1, 2, 3]):
                            total = total + taps_ref[level, 7 + column, span, :] * pltpu.roll(
                                mid, (-d) % lanes, 1
                            )
                        v_ref[span, pl.ds(r * lanes, lanes)] = total
                        square = total * total
                        small[r] = total if small[r] is None else small[r] + total
                        small[2 + r] = square if small[2 + r] is None else small[2 + r] + square
                for i in range(4):
                    sums[i] = sums[i] + small[i].astype(F32)
            scales = []
            for r in range(2):
                mean = jnp.sum(sums[r], axis=0, keepdims=True) * (1.0 / channels)
                second = jnp.sum(sums[2 + r], axis=0, keepdims=True) * (1.0 / channels)
                variance = jnp.maximum(second - mean * mean, 0.0)
                row = first + REACH * (level + 1) + k + r
                inside = jnp.logical_and(row >= 0, row < height)
                scales.append(jnp.where(inside, 0.5 * lax.rsqrt(variance + epsilon), 0.0))
            scale = jnp.concatenate(scales, axis=1)
            acc_ref[...] = jnp.dot(mix_ref[level], v_ref[...], preferred_element_type=F32)
            for b in range(blocks):
                span = pl.ds(b * group, group)
                half = (acc_ref[span, :] * scale).astype(BF16)
                inner = half * (half * half * c1 + c0)
                gate = half + half * jnp.tanh(inner)
                for r in range(2):
                    h_ref[k + r, span, :] = (
                        h_ref[k + REACH + r, span, :] + gate[:, r * lanes : (r + 1) * lanes]
                    )
            return 0

        lax.fori_loop(0, out_rows // 2, pair, 0)
        return 0

    lax.fori_loop(0, layers, layer, 0)

    dec = dec_ref[...]

    def decode(k, _):
        h = jnp.concatenate([h_ref[2 * k], h_ref[2 * k + 1]], axis=1)
        y = jnp.dot(dec, h, preferred_element_type=F32)
        for r in range(2):
            row = 2 * k + r
            base = own_ref[row, :variables].astype(F32)
            out_ref[row, :variables] = (base + y[:, r * lanes : (r + 1) * lanes]).astype(BF16)
            if carry_noise:
                out_ref[row, variables:] = own_ref[row, inputs:]
        return 0

    lax.fori_loop(0, own // 2, decode, 0)


def rollout_step(up, own, down, enc, taps, mix, dec, carry_noise):
    layers, channels = mix.shape[0], mix.shape[1]
    variables = dec.shape[0]
    rows, lanes = own.shape[0], own.shape[2]
    total = rows + 2 * up.shape[0]
    out_channels = enc.shape[1] if carry_noise else variables
    return pl.pallas_call(
        functools.partial(step_kernel, layers, variables, carry_noise),
        out_shape=jax.ShapeDtypeStruct((rows, out_channels, lanes), BF16),
        in_specs=[pl.BlockSpec(memory_space=pltpu.VMEM)] * 7,
        out_specs=pl.BlockSpec(memory_space=pltpu.VMEM),
        scratch_shapes=[
            pltpu.VMEM((total, channels, lanes), BF16),
            pltpu.VMEM((channels, 2 * lanes), BF16),
            pltpu.VMEM((channels, 2 * lanes), F32),
        ],
        compiler_params=pltpu.CompilerParams(vmem_limit_bytes=48 * 1024 * 1024),
        name="rollout_step",
    )(up, own, down, enc, taps, mix, dec)


def z_shift(block, reach, bands):
    pairs = [(i, i + reach) for i in range(bands) if 0 <= i + reach < bands]
    return lax.ppermute(block, "lat", pairs)


def local(
    state, noise, target, encoder_state_weight, enc_noise, lat_taps, lon_taps, gains, mix, decode
):
    variables, rows_dev, cols_dev = state.shape
    layers, channels = mix.shape[0], mix.shape[1]
    noise_count = noise.shape[2]
    inputs = variables + noise_count
    bands = lax.axis_size("lat")
    halo = REACH * layers
    side = 2 * halo
    core = lax.axis_index("lat") % 2
    sibling = [(i, i ^ 1) for i in range(bands)]

    gathered = jnp.concatenate([state, noise[0, 0], noise[0, 1]], axis=0)
    mine = jnp.transpose(gathered, (1, 0, 2))
    other = lax.ppermute(mine, "lat", sibling)
    low = jnp.where(core == 0, mine, other)
    high = jnp.where(core == 0, other, mine)
    block = jnp.concatenate([low, high], axis=0)
    rows = block.shape[0]
    right = block[:, :, cols_dev - side :]
    left = block[:, :, :side]
    edge = jnp.where(core == 0, right, left).reshape(4, rows // 4, -1, side)
    packed = jnp.concatenate([edge[i] for i in range(4)], axis=-1)
    packed = lax.ppermute(packed, "lon", [(0, 1), (1, 0)])
    edge = jnp.concatenate([packed[:, :, i * side : (i + 1) * side] for i in range(4)], axis=0)
    block = jnp.concatenate(
        [
            jnp.where(core == 1, edge, left),
            block[:, :, side : cols_dev - side],
            jnp.where(core == 0, edge, right),
        ],
        axis=-1,
    )
    up = z_shift(block[rows - halo :, :inputs], 2, bands)
    down = z_shift(block[:halo, :inputs], -2, bands)

    enc = jnp.concatenate([encoder_state_weight, enc_noise], axis=1)
    taps = jnp.concatenate([lat_taps, lon_taps], axis=1).astype(BF16)
    taps = jnp.broadcast_to(taps[..., None], taps.shape + (cols_dev,))
    scaled = mix.astype(F32) * gains[:, None, :]
    scaled = (scaled - jnp.mean(scaled, axis=2, keepdims=True)).astype(BF16)

    first = rollout_step(up, block, down, enc, taps, scaled, decode, True)
    up = z_shift(first[rows - halo :], 2, bands)
    down = z_shift(first[:halo], -2, bands)
    second = rollout_step(up, first, down, enc, taps, scaled, decode, False)

    both = jnp.stack([first[:, :variables], second])
    lower = both[:, :rows_dev]
    upper = both[:, rows_dev:]
    kept = jnp.where(core == 0, lower, upper)
    sent = jnp.where(core == 0, upper, lower)
    taken = lax.ppermute(sent, "lat", sibling)
    lane = lax.broadcasted_iota(jnp.int32, kept.shape, 3)
    keep = (lane >= cols_dev // 2) == (core == 1)
    merged = jnp.where(keep, kept, taken)
    trajectory_predictions = jnp.transpose(merged, (0, 2, 1, 3))[None]

    members = lax.axis_size("member")
    scale = float(members)
    regrouped = lax.all_to_all(
        trajectory_predictions, "member", split_axis=2, concat_axis=0, tiled=True
    )
    quantities_real = regrouped.astype(F32)
    part = variables // members
    start = lax.axis_index("member") * part
    target_block = lax.dynamic_slice_in_dim(target, start, part, 1).astype(F32)
    skill = jnp.sum(jnp.abs(quantities_real - target_block[None]), axis=(0, 1))
    spread = jnp.zeros(skill.shape, F32)
    for i in range(members):
        for j in range(i):
            spread = spread + jnp.sum(jnp.abs(quantities_real[i] - quantities_real[j]), axis=0)
    probabilistic_error = skill / scale - spread / (scale * (scale - 1.0))
    return (trajectory_predictions, probabilistic_error)


def solution(mesh):
    in_specs = (
        P(None, "lat", "lon"),
        P("member", None, None, "lat", "lon"),
        P(None, None, "lat", "lon"),
        P(),
        P(),
        P(),
        P(),
        P(),
        P(),
        P(),
    )
    out_specs = (P("member", None, None, "lat", "lon"), P("member", "lat", "lon"))
    return jax.shard_map(local, mesh=mesh, in_specs=in_specs, out_specs=out_specs, check_vma=False)
```

profile of v0, /device:TPU:32, one launch (start us, length us, event | category | flops | bytes accessed | tf_op | source)
XLA Modules:
  0.0 186.7 jit_solution(18134366768968922462)
XLA Ops:
  0.6 0.7 fusion.17
  1.4 0.9 copy.45
  2.3 0.1 collective-permute-start
  2.5 0.8 convert.8
  3.3 0.8 convert.9
  4.2 1.0 copy.46
  5.2 0.9 copy.47
  6.1 2.1 %fusion = f32[4,512]{1,0:T(4,128)S(1)} fusion(bf16[4,512,512]{2,1,0:T(8,128)(2,1)} %param.18, f32[4,512]{1,0:T(4,128)} %param.17), kind=kLoop, calls=%fused_computation.2 | loop fusion | flops 3143680 | bytes 2113536 | tf_op jit(solution)/shard_map/reduce_sum | solution.py:199
  8.1 0.0 copy-start.1
  8.2 0.0 copy-start.2
  8.2 0.0 collective-permute-done
  8.2 0.1 broadcast_select_fusion.4
  8.3 0.2 broadcast_select_fusion.1
  8.5 0.1 pad_maximum_fusion.3
  8.6 1.6 collective-permute-start.1
  10.2 0.1 pad_maximum_fusion.2.enc_ref
  10.3 3.4 %collective-permute-done.1 = bf16[4,88,96]{2,1,0:T(8,128)(2,1)S(1)} collective-permute-done((bf16[4,88,96]{2,1,0:T(8,128)(2,1)S(1)}, bf16[4,88,96]{2,1,0:T(8,128)(2,1)S(1)}, u32[]{:S(2)}, u32[]{:S(2)}) %collective-permute-start.1) | collective-permute-done | bytes 67616 | tf_op jit(solution)/shard_map/ppermute | solution.py:182
  13.7 0.1 fusion.16
  13.9 0.2 broadcast_select_fusion.2
  14.1 0.3 fusion.11.own_ref
  14.4 0.1 fusion.13
  14.5 3.8 %collective-permute-start.2 = (bf16[12,80,128]{2,1,0:T(8,128)(2,1)S(1)}, bf16[12,80,128]{2,1,0:T(8,128)(2,1)S(1)}, u32[]{:S(2)}, u32[]{:S(2)}) collective-permute-start(bf16[12,80,128]{2,1,0:T(8,128)(2,1)S(1)} %get-tuple-element.50), channel_id=1, source_target_pairs={{0,4},{2,6},{4,8},{6,10},{8,12},{10,14},{12,16},{14,18},{16,20},{1... | collective-permute-start | bytes 737288 | tf_op jit(solution)/shard_map/ppermute | solution.py:155
  18.3 2.0 %collective-permute-start.3 = (bf16[12,80,128]{2,1,0:T(8,128)(2,1)S(1)}, bf16[12,80,128]{2,1,0:T(8,128)(2,1)S(1)}, u32[]{:S(2)}, u32[]{:S(2)}) collective-permute-start(bf16[12,80,128]{2,1,0:T(8,128)(2,1)S(1)} %get-tuple-element.49), channel_id=1, source_target_pairs={{4,0},{6,2},{8,4},{10,6},{12,8},{14,10},{16,12},{18,14},{20,16},{2... | collective-permute-start | bytes 737288 | tf_op jit(solution)/shard_map/ppermute | solution.py:155
  20.3 0.0 copy-done.1
  20.4 0.0 copy-done.2
  20.4 0.6 subtract_convert_fusion.mix_ref
  20.9 0.0 copy-start
  20.9 2.9 %collective-permute-done.2.up_ref = bf16[12,80,128]{2,1,0:T(8,128)(2,1)S(1)} collective-permute-done((bf16[12,80,128]{2,1,0:T(8,128)(2,1)S(1)}, bf16[12,80,128]{2,1,0:T(8,128)(2,1)S(1)}, u32[]{:S(2)}, u32[]{:S(2)}) %collective-permute-start.2) | collective-permute-done | bytes 245792 | tf_op jit(solution)/shard_map/ppermute | solution.py:155
  23.9 3.7 %collective-permute-done.3.down_ref = bf16[12,80,128]{2,1,0:T(8,128)(2,1)S(1)} collective-permute-done((bf16[12,80,128]{2,1,0:T(8,128)(2,1)S(1)}, bf16[12,80,128]{2,1,0:T(8,128)(2,1)S(1)}, u32[]{:S(2)}, u32[]{:S(2)}) %collective-permute-start.3) | collective-permute-done | bytes 245792 | tf_op jit(solution)/shard_map/ppermute | solution.py:155
  27.6 6.3 %broadcast_in_dim.4.taps_ref = bf16[4,13,512,128]{3,2,1,0:T(8,128)(2,1)} broadcast(bf16[4,13,512]{2,1,0:T(8,128)(2,1)S(1)} %copy.48), dimensions={0,1,2} | broadcast | bytes 6868992 | tf_op jit(solution)/shard_map/broadcast_in_dim | solution.py:197
  33.9 0.0 copy-done
  33.9 59.3 %rollout_step.2.own_ref = bf16[16,80,128]{2,1,0:T(8,128)(2,1)S(1)} custom-call(bf16[12,80,128]{2,1,0:T(8,128)(2,1)S(1)} %collective-permute-done.2.up_ref, bf16[16,88,128]{2,1,0:T(8,128)(2,1)S(1)} %fusion.11.own_ref, bf16[12,80,128]{2,1,0:T(8,128)(2,1)S(1)} %collective-permute-done.3.down_ref, bf16[512,80]{1,0:T(8,128)(2,1)S(1)} %pad_maximum_fusion.2.enc_ref, ...), custom_call_target="tpu_custom_call" | custom-call | tf_op jit(solution)/shard_map/rollout_step/pallas_call | solution.py:138
  93.2 0.1 fusion.15
  93.3 5.1 %collective-permute-start.4 = (bf16[12,80,128]{2,1,0:T(8,128)(2,1)S(1)}, bf16[12,80,128]{2,1,0:T(8,128)(2,1)S(1)}, u32[]{:S(2)}, u32[]{:S(2)}) collective-permute-start(bf16[12,80,128]{2,1,0:T(8,128)(2,1)S(1)} %get-tuple-element.58), channel_id=1, source_target_pairs={{0,4},{2,6},{4,8},{6,10},{8,12},{10,14},{12,16},{14,18},{16,20},{1... | collective-permute-start | bytes 737288 | tf_op jit(solution)/shard_map/ppermute | solution.py:155
  98.3 1.9 %collective-permute-start.5 = (bf16[12,80,128]{2,1,0:T(8,128)(2,1)S(1)}, bf16[12,80,128]{2,1,0:T(8,128)(2,1)S(1)}, u32[]{:S(2)}, u32[]{:S(2)}) collective-permute-start(bf16[12,80,128]{2,1,0:T(8,128)(2,1)S(1)} %get-tuple-element.57), channel_id=1, source_target_pairs={{4,0},{6,2},{8,4},{10,6},{12,8},{14,10},{16,12},{18,14},{20,16},{2... | collective-permute-start | bytes 737288 | tf_op jit(solution)/shard_map/ppermute | solution.py:155
  100.3 2.2 %collective-permute-done.4.up_ref = bf16[12,80,128]{2,1,0:T(8,128)(2,1)S(1)} collective-permute-done((bf16[12,80,128]{2,1,0:T(8,128)(2,1)S(1)}, bf16[12,80,128]{2,1,0:T(8,128)(2,1)S(1)}, u32[]{:S(2)}, u32[]{:S(2)}) %collective-permute-start.4) | collective-permute-done | bytes 245792 | tf_op jit(solution)/shard_map/ppermute | solution.py:155
  102.4 5.0 %collective-permute-done.5.down_ref = bf16[12,80,128]{2,1,0:T(8,128)(2,1)S(1)} collective-permute-done((bf16[12,80,128]{2,1,0:T(8,128)(2,1)S(1)}, bf16[12,80,128]{2,1,0:T(8,128)(2,1)S(1)}, u32[]{:S(2)}, u32[]{:S(2)}) %collective-permute-start.5) | collective-permute-done | bytes 245792 | tf_op jit(solution)/shard_map/ppermute | solution.py:155
  107.5 59.3 %rollout_step.3 = bf16[16,72,128]{2,1,0:T(8,128)(2,1)S(1)} custom-call(bf16[12,80,128]{2,1,0:T(8,128)(2,1)S(1)} %collective-permute-done.4.up_ref, bf16[16,80,128]{2,1,0:T(8,128)(2,1)S(1)} %rollout_step.2.own_ref, bf16[12,80,128]{2,1,0:T(8,128)(2,1)S(1)} %collective-permute-done.5.down_ref, bf16[512,80]{1,0:T(8,128)(2,1)S(1)} %pad_maximum_fusion.2.enc_ref, ...), custom_call_target="tpu_custom_call" | custom-call | tf_op jit(solution)/shard_map/rollout_step/pallas_call | solution.py:138
  166.8 0.1 broadcast_select_fusion.3
  166.8 0.1 collective-permute-start.6
  167.0 1.6 collective-permute-done.6
  168.5 0.1 select_bitcast_fusion
  168.6 0.7 copy.49
  169.3 6.9 %all-to-all-start = ((bf16[1,2,72,8,128]{4,3,1,0,2:T(8,128)(2,1)}), bf16[1,2,72,8,128]{4,3,1,0,2:T(8,128)(2,1)S(1)}, u32[]{:S(2)}, u32[]{:S(2)}) async-start(bf16[1,2,72,8,128]{4,3,1,0,2:T(8,128)(2,1)} %copy.49), calls=%async_computation | async-start | bytes 589824 | tf_op jit(solution)/shard_map/all_to_all | solution.py:219
  176.2 0.8 dynamic-slice_convert_fusion
  177.0 0.8 copy.51
  177.8 7.8 %all-to-all-done = bf16[1,2,72,8,128]{4,3,1,0,2:T(8,128)(2,1)S(1)} async-done(((bf16[1,2,72,8,128]{4,3,1,0,2:T(8,128)(2,1)}), bf16[1,2,72,8,128]{4,3,1,0,2:T(8,128)(2,1)S(1)}, u32[]{:S(2)}, u32[]{:S(2)}) %all-to-all-start) | async-done | bytes 294944 | tf_op jit(solution)/shard_map/all_to_all | solution.py:219
  185.6 0.2 abs_reduce_fusion.26
  185.8 0.1 abs_reduce_fusion.25
  185.9 0.1 fusion.4
  186.0 0.7 multiply_subtract_fusion
  (10 shorter events, 0.2 us)
Async XLA Ops:
  2.3 5.8 %collective-permute-start = (bf16[8,88,128]{2,1,0:T(8,128)(2,1)S(1)}, bf16[8,88,128]{2,1,0:T(8,128)(2,1)S(1)}, u32[]{:S(2)}, u32[]{:S(2)}) collective-permute-start(bf16[8,88,128]{2,1,0:T(8,128)(2,1)S(1)} %maximum_bitcast_fusion), channel_id=1, source_target_pairs={{0,2},{2,0},{4,6},{6,4},{8,10},{10,8},{12,14},{14,12},{16,18},{18,... | collective-permute-start | bytes 540680 | tf_op jit(solution)/shard_map/ppermute | solution.py:173
  8.1 12.2 %copy-start.1 = (bf16[4,512,512]{2,1,0:T(8,128)(2,1)S(1)}, bf16[4,512,512]{2,1,0:T(8,128)(2,1)}, u32[]{:S(2)}) copy-start(bf16[4,512,512]{2,1,0:T(8,128)(2,1)} %param.18) | copy-start | bytes 6291460
  8.2 12.2 %copy-start.2 = (f32[4,512]{1,0:T(4,128)S(1)}, f32[4,512]{1,0:T(4,128)}, u32[]{:S(2)}) copy-start(f32[4,512]{1,0:T(4,128)} %param.17) | copy-start | bytes 24580
  8.6 5.1 %collective-permute-start.1 = (bf16[4,88,96]{2,1,0:T(8,128)(2,1)S(1)}, bf16[4,88,96]{2,1,0:T(8,128)(2,1)S(1)}, u32[]{:S(2)}, u32[]{:S(2)}) collective-permute-start(bf16[4,88,96]{2,1,0:T(8,128)(2,1)S(1)} %pad_maximum_fusion.3), channel_id=1, source_target_pairs={{0,1},{1,0},{2,3},{3,2},{4,5},{5,4},{6,7},{7,6},{8,9},{9,8},{10,11... | collective-permute-start | bytes 202760 | tf_op jit(solution)/shard_map/ppermute | solution.py:182
  14.5 9.4 %collective-permute-start.2 = (bf16[12,80,128]{2,1,0:T(8,128)(2,1)S(1)}, bf16[12,80,128]{2,1,0:T(8,128)(2,1)S(1)}, u32[]{:S(2)}, u32[]{:S(2)}) collective-permute-start(bf16[12,80,128]{2,1,0:T(8,128)(2,1)S(1)} %get-tuple-element.50), channel_id=1, source_target_pairs={{0,4},{2,6},{4,8},{6,10},{8,12},{10,14},{12,16},{14,18},{16,20},{1... | collective-permute-start | bytes 737288 | tf_op jit(solution)/shard_map/ppermute | solution.py:155
  18.3 9.3 %collective-permute-start.3 = (bf16[12,80,128]{2,1,0:T(8,128)(2,1)S(1)}, bf16[12,80,128]{2,1,0:T(8,128)(2,1)S(1)}, u32[]{:S(2)}, u32[]{:S(2)}) collective-permute-start(bf16[12,80,128]{2,1,0:T(8,128)(2,1)S(1)} %get-tuple-element.49), channel_id=1, source_target_pairs={{4,0},{6,2},{8,4},{10,6},{12,8},{14,10},{16,12},{18,14},{20,16},{2... | collective-permute-start | bytes 737288 | tf_op jit(solution)/shard_map/ppermute | solution.py:155
  20.9 13.0 %copy-start = (bf16[72,512]{1,0:T(8,128)(2,1)S(1)}, bf16[72,512]{1,0:T(8,128)(2,1)}, u32[]{:S(2)}) copy-start(bf16[72,512]{1,0:T(8,128)(2,1)} %dec_ref.3) | copy-start | bytes 221188
  93.3 9.2 %collective-permute-start.4 = (bf16[12,80,128]{2,1,0:T(8,128)(2,1)S(1)}, bf16[12,80,128]{2,1,0:T(8,128)(2,1)S(1)}, u32[]{:S(2)}, u32[]{:S(2)}) collective-permute-start(bf16[12,80,128]{2,1,0:T(8,128)(2,1)S(1)} %get-tuple-element.58), channel_id=1, source_target_pairs={{0,4},{2,6},{4,8},{6,10},{8,12},{10,14},{12,16},{14,18},{16,20},{1... | collective-permute-start | bytes 737288 | tf_op jit(solution)/shard_map/ppermute | solution.py:155
  98.3 9.2 %collective-permute-start.5 = (bf16[12,80,128]{2,1,0:T(8,128)(2,1)S(1)}, bf16[12,80,128]{2,1,0:T(8,128)(2,1)S(1)}, u32[]{:S(2)}, u32[]{:S(2)}) collective-permute-start(bf16[12,80,128]{2,1,0:T(8,128)(2,1)S(1)} %get-tuple-element.57), channel_id=1, source_target_pairs={{4,0},{6,2},{8,4},{10,6},{12,8},{14,10},{16,12},{18,14},{20,16},{2... | collective-permute-start | bytes 737288 | tf_op jit(solution)/shard_map/ppermute | solution.py:155
  166.8 1.7 collective-permute-start.6
  169.3 16.2 %all-to-all-start = ((bf16[1,2,72,8,128]{4,3,1,0,2:T(8,128)(2,1)}), bf16[1,2,72,8,128]{4,3,1,0,2:T(8,128)(2,1)S(1)}, u32[]{:S(2)}, u32[]{:S(2)}) async-start(bf16[1,2,72,8,128]{4,3,1,0,2:T(8,128)(2,1)} %copy.49), calls=%async_computation | async-start | bytes 589824 | tf_op jit(solution)/shard_map/all_to_all | solution.py:219
where the time goes:
time: 187 us
  Pallas kernels  119 us (64%)
  waiting for transfers between devices  26.6 us (14%)
  starting transfers between devices  21.5 us (11%)
  local copies, waits for them, and re-layouts  11.7 us (6%)
  other arithmetic  7.37 us (4%)
    pallas_call x2, Pallas kernels, rollout_step(): pl.pallas_call(functools.partial(step_kernel, layers, variables, carry_no...  119 us
    ppermute x4, waiting for transfers between devices, z_shift(): return lax.ppermute(block, 'lat', pairs)  13.9 us
    ppermute x4, starting transfers between devices, z_shift(): return lax.ppermute(block, 'lat', pairs)  12.8 us
    all_to_all x1, waiting for transfers between devices, local(): lax.all_to_all(trajectory_predictions, 'member', split_axis=2, concat_axi...  7.8 us
    all_to_all x1, starting transfers between devices, local(): lax.all_to_all(trajectory_predictions, 'member', split_axis=2, concat_axi...  6.92 us
    broadcast_in_dim x1, local copies, waits for them, and re-layouts, local(): taps = jnp.broadcast_to(taps[..., None], taps.shape + (cols_dev,))  6.31 us
  transfers between devices with their start and end apart: 8, of which 7 were waited for; matrix products, arithmetic and copies ran while one was open for 4% of the time, Pallas kernels for 0%

commit v1 on v0

v1 whole, which is shorter than its diff:
```python
import functools

import jax
import jax.numpy as jnp
from jax import lax
from jax.experimental import pallas as pl
from jax.experimental.pallas import tpu as pltpu
from jax.sharding import PartitionSpec as P

epsilon = 1e-05
REACH = 3
F32 = jnp.float32
BF16 = jnp.bfloat16


def step_kernel(
    width,
    up_ref,
    own_ref,
    down_ref,
    enc_ref,
    taps_ref,
    mix_ref,
    dec_ref,
    out_ref,
    h_ref,
    v_ref,
    acc_ref,
    scale_ref,
):
    halo = up_ref.shape[0]
    own = own_ref.shape[0]
    planes, _, _, lanes = h_ref.shape
    span = own_ref.shape[2]
    channels = planes * lanes
    inputs = enc_ref.shape[0]
    layers = mix_ref.shape[0]
    variables = dec_ref.shape[0]
    position = lax.axis_index("lat")
    band = position // 2
    first = band * own - halo
    height = (lax.axis_size("lat") // 2) * own
    margin = (width - span // 2) // 2
    inset = -margin % 8
    start = jnp.where(
        position % 2 == 0, span - margin - inset, span // 2 - margin - inset
    )

    def encode(source, offset):
        def one(k, _):
            y = lax.dot_general(
                source[k, :inputs],
                enc_ref[...],
                (((0,), (0,)), ((), ())),
                preferred_element_type=F32,
            )
            for chunk in range(span // 8):
                place = pl.multiple_of(8 + lax.rem(8 * chunk - start + span, span), 8)
                for t in range(planes):
                    h_ref[t, offset + k, pl.ds(place, 8), :] = y[
                        8 * chunk : 8 * chunk + 8, t * lanes : (t + 1) * lanes
                    ]
            return 0

        lax.fori_loop(0, source.shape[0], one, 0)

    encode(up_ref, 0)
    encode(own_ref, halo)
    encode(down_ref, halo + own)

    c0 = 2.0 * 0.7978845608028654
    c1 = 8.0 * 0.7978845608028654 * 0.044715

    for level in range(layers):
        edge = REACH * (level + 1)
        left = (inset + edge) // 8 * 8
        tiles = -(-(inset + width - edge - left) // 16)
        groups = -(-(own + 2 * halo - 2 * edge) // 4)

        def group(g, _, level=level, edge=edge, tiles=tiles, left=left + 8):
            k = 4 * g

            def convolve(j, _):
                c = pl.multiple_of(left + 16 * j, 8)
                for t in range(planes):
                    part = slice(t * lanes, (t + 1) * lanes)
                    rows = [h_ref[t, k + i, pl.ds(c, 16), :].astype(BF16) for i in range(10)]
                    totals = [None] * 4
                    for d in range(7):
                        tap = taps_ref[level, d, :, part]
                        for r in range(4):
                            term = rows[r + d] * tap
                            totals[r] = term if d == 0 else totals[r] + term
                    for column, d in enumerate([-3, -2, -1, 1, 2, 3]):
                        tap = taps_ref[level, 7 + column, :, part]
                        for r in range(4):
                            shifted = h_ref[t, k + r + REACH, pl.ds(c + d, 16), :].astype(BF16)
                            totals[r] = totals[r] + shifted * tap
                    for r in range(4):
                        m = pl.multiple_of(r * 16 * tiles + 16 * j, 16)
                        v_ref[pl.ds(m, 16), part] = totals[r]
                return 0

            lax.fori_loop(0, tiles, convolve, 0)
            size = 64 * tiles
            acc_ref[:size] = jnp.dot(
                v_ref[:size], mix_ref[level], preferred_element_type=F32
            )
            for r in range(4):
                row = first + edge + k + r
                inside = jnp.logical_and(row >= 0, row < height).astype(F32)
                for j in range(tiles):
                    m = r * 16 * tiles + 16 * j
                    parts = [
                        v_ref[m : m + 16, t * lanes : (t + 1) * lanes] for t in range(planes)
                    ]
                    total = functools.reduce(jnp.add, parts).astype(F32)
                    square = functools.reduce(jnp.add, [x * x for x in parts]).astype(F32)
                    mean = jnp.sum(total, axis=1, keepdims=True)
                    second = jnp.sum(square, axis=1, keepdims=True)
                    variance = jnp.maximum(
                        second * (1.0 / channels) - mean * mean * (1.0 / channels**2), 0.0
                    )
                    scale = lax.rsqrt(variance + epsilon) * inside
                    scale_ref[m : m + 16, :] = jnp.broadcast_to(scale, (16, lanes))
            for j in range(tiles):
                c = left + 16 * j
                for r in range(4):
                    m = r * 16 * tiles + 16 * j
                    scale = scale_ref[m : m + 16, :].astype(BF16)
                    for t in range(planes):
                        part = slice(t * lanes, (t + 1) * lanes)
                        half = acc_ref[m : m + 16, part].astype(BF16) * scale
                        inner = half * (half * half * c1 + c0)
                        gate = half + half * jnp.tanh(inner)
                        h_ref[t, k + r, c : c + 16, :] = h_ref[
                            t, k + REACH + r, c : c + 16, :
                        ] + gate.astype(F32)
            return 0

        lax.fori_loop(0, groups, group, 0)

    def decode(k, _):
        h = jnp.concatenate([h_ref[t, k, pl.ds(8, span), :] for t in range(planes)], axis=1).astype(BF16)
        y = lax.dot_general(
            dec_ref[...], h, (((1,), (1,)), ((), ())), preferred_element_type=F32
        )
        y = pltpu.roll(y, start, 1)
        out_ref[k, :variables] = (own_ref[k, :variables].astype(F32) + y).astype(BF16)
        if out_ref.shape[1] > variables:
            out_ref[k, variables:] = own_ref[k, inputs:]
        return 0

    lax.fori_loop(0, own, decode, 0)


def rollout_step(up, own, down, enc, taps, mix, dec, width, carry_noise):
    channels = mix.shape[1]
    variables = dec.shape[0]
    rows, lanes = own.shape[0], own.shape[2]
    total = rows + 2 * up.shape[0] + 4
    cells = 64 * (-(-(width - 2 * REACH) // 16))
    out_channels = enc.shape[0] if carry_noise else variables
    return pl.pallas_call(
        functools.partial(step_kernel, width),
        out_shape=jax.ShapeDtypeStruct((rows, out_channels, lanes), BF16),
        in_specs=[pl.BlockSpec(memory_space=pltpu.VMEM)] * 7,
        out_specs=pl.BlockSpec(memory_space=pltpu.VMEM),
        scratch_shapes=[
            pltpu.VMEM((channels // lanes, total, lanes + 24, lanes), F32),
            pltpu.VMEM((cells, channels), BF16),
            pltpu.VMEM((cells, channels), F32),
            pltpu.VMEM((cells, lanes), F32),
        ],
        compiler_params=pltpu.CompilerParams(vmem_limit_bytes=48 * 1024 * 1024),
        name="rollout_step",
    )(up, own, down, enc, taps, mix, dec)


def z_shift(block, reach, bands):
    pairs = [(i, i + reach) for i in range(bands) if 0 <= i + reach < bands]
    return lax.ppermute(block, "lat", pairs)


def local(
    state, noise, target, encoder_state_weight, enc_noise, lat_taps, lon_taps, gains, mix, decode
):
    variables, rows_dev, cols_dev = state.shape
    layers, channels = mix.shape[0], mix.shape[1]
    noise_count = noise.shape[2]
    inputs = variables + noise_count
    bands = lax.axis_size("lat")
    halo = REACH * layers
    side = 2 * halo
    core = lax.axis_index("lat") % 2
    sibling = [(i, i ^ 1) for i in range(bands)]

    gathered = jnp.concatenate([state, noise[0, 0], noise[0, 1]], axis=0)
    mine = jnp.transpose(gathered, (1, 0, 2))
    other = lax.ppermute(mine, "lat", sibling)
    low = jnp.where(core == 0, mine, other)
    high = jnp.where(core == 0, other, mine)
    block = jnp.concatenate([low, high], axis=0)
    rows = block.shape[0]
    right = block[:, :, cols_dev - side :]
    left = block[:, :, :side]
    edge = jnp.where(core == 0, right, left).reshape(4, rows // 4, -1, side)
    packed = jnp.concatenate([edge[i] for i in range(4)], axis=-1)
    packed = lax.ppermute(packed, "lon", [(0, 1), (1, 0)])
    edge = jnp.concatenate([packed[:, :, i * side : (i + 1) * side] for i in range(4)], axis=0)
    block = jnp.concatenate(
        [
            jnp.where(core == 1, edge, left),
            block[:, :, side : cols_dev - side],
            jnp.where(core == 0, edge, right),
        ],
        axis=-1,
    )
    up = z_shift(block[rows - halo :, :inputs], 2, bands)
    down = z_shift(block[:halo, :inputs], -2, bands)

    enc = jnp.concatenate([encoder_state_weight, enc_noise], axis=1).T
    taps = jnp.concatenate([lat_taps, lon_taps], axis=1).astype(BF16)
    taps = jnp.broadcast_to(taps[:, :, None, :], taps.shape[:2] + (16, channels))
    scaled = mix.astype(F32) * (0.5 * gains[:, None, :])
    scaled = (scaled - jnp.mean(scaled, axis=2, keepdims=True)).astype(BF16)
    scaled = jnp.transpose(scaled, (0, 2, 1))

    first = rollout_step(up, block, down, enc, taps, scaled, decode, cols_dev // 2 + 2 * side, True)
    up = z_shift(first[rows - halo :], 2, bands)
    down = z_shift(first[:halo], -2, bands)
    second = rollout_step(up, first, down, enc, taps, scaled, decode, cols_dev // 2 + side, False)

    both = jnp.stack([first[:, :variables], second])
    lower = both[:, :rows_dev]
    upper = both[:, rows_dev:]
    kept = jnp.where(core == 0, lower, upper)
    sent = jnp.where(core == 0, upper, lower)
    taken = lax.ppermute(sent, "lat", sibling)
    lane = lax.broadcasted_iota(jnp.int32, kept.shape, 3)
    keep = (lane >= cols_dev // 2) == (core == 1)
    merged = jnp.where(keep, kept, taken)
    trajectory_predictions = jnp.transpose(merged, (0, 2, 1, 3))[None]

    members = lax.axis_size("member")
    scale = float(members)
    regrouped = lax.all_to_all(
        trajectory_predictions, "member", split_axis=2, concat_axis=0, tiled=True
    )
    quantities_real = regrouped.astype(F32)
    part = variables // members
    start = lax.axis_index("member") * part
    target_block = lax.dynamic_slice_in_dim(target, start, part, 1).astype(F32)
    skill = jnp.sum(jnp.abs(quantities_real - target_block[None]), axis=(0, 1))
    spread = jnp.zeros(skill.shape, F32)
    for i in range(members):
        for j in range(i):
            spread = spread + jnp.sum(jnp.abs(quantities_real[i] - quantities_real[j]), axis=0)
    probabilistic_error = skill / scale - spread / (scale * (scale - 1.0))
    return (trajectory_predictions, probabilistic_error)


def solution(mesh):
    in_specs = (
        P(None, "lat", "lon"),
        P("member", None, None, "lat", "lon"),
        P(None, None, "lat", "lon"),
        P(),
        P(),
        P(),
        P(),
        P(),
        P(),
        P(),
    )
    out_specs = (P("member", None, None, "lat", "lon"), P("member", "lat", "lon"))
    return jax.shard_map(local, mesh=mesh, in_specs=in_specs, out_specs=out_specs, check_vma=False)
```

time: 187 us -> 135 us (0.72)
  Pallas kernels: 119 us -> 74.6 us
  local copies, waits for them, and re-layouts: 11.7 us -> 6.44 us
  other arithmetic: 7.37 us -> 4.06 us
    pallas_call x2, Pallas kernels: 119 us -> 74.6 us  [rollout_step(): pl.pallas_call(functools.partial(step_kernel, width), out_shape=jax.Shape...]
    broadcast_in_dim x1, local copies, waits for them, and re-layouts: 6.31 us -> 0.07 us  [local(): jnp.broadcast_to(taps[:, :, None, :], taps.shape[:2] + (16, channels))]
    unnamed x10 -> x15, local copies, waits for them, and re-layouts: 3.56 us -> 4.54 us
where the time goes in v1:
time: 135 us; the launch traced here: 134 us
  Pallas kernels  74.6 us (55%)
  waiting for transfers between devices  26.6 us (20%)
  starting transfers between devices  21.6 us (16%)
  local copies, waits for them, and re-layouts  6.44 us (5%)
  other arithmetic  4.06 us (3%)
    pallas_call x2, Pallas kernels, rollout_step(): pl.pallas_call(functools.partial(step_kernel, width), out_shape=jax.Shape...  74.6 us
    ppermute x4, waiting for transfers between devices, z_shift(): return lax.ppermute(block, 'lat', pairs)  13.8 us
    ppermute x4, starting transfers between devices, z_shift(): return lax.ppermute(block, 'lat', pairs)  12.9 us
    all_to_all x1, waiting for transfers between devices, local(): lax.all_to_all(trajectory_predictions, 'member', split_axis=2, concat_axi...  7.8 us
    all_to_all x1, starting transfers between devices, local(): lax.all_to_all(trajectory_predictions, 'member', split_axis=2, concat_axi...  6.93 us
    unnamed x15, local copies, waits for them, and re-layouts  4.54 us
    ppermute x1, waiting for transfers between devices, local(): packed = lax.ppermute(packed, 'lon', [(0, 1), (1, 0)])  3.46 us
  transfers between devices with their start and end apart: 8, of which 7 were waited for; matrix products, arithmetic and copies ran while one was open for 4% of the time, Pallas kernels for 0%

profile of v1, /device:TPU:32, one launch (start us, length us, event | category | flops | bytes accessed | tf_op | source)
XLA Modules:
  0.0 134.4 jit_solution(14834559719306013060)
XLA Ops:
  0.6 0.7 fusion.18
  1.4 0.9 copy.42
  2.3 0.1 collective-permute-start
  2.5 0.0 copy-start.5
  2.5 0.0 copy-start.2
  2.5 0.0 copy-start.3
  2.5 2.8 %copy.44 = bf16[4,512,512]{1,2,0:T(8,128)(2,1)S(1)} copy(bf16[4,512,512]{2,1,0:T(8,128)(2,1)} %param.18) | data formatting | bytes 4194304 | tf_op args[8]
  5.3 0.0 copy-done.5
  5.3 0.0 copy-done.2
  5.4 0.0 copy-done.3
  5.5 0.0 copy-start.1
  5.5 0.0 copy-start.4
  5.5 0.5 fusion
  6.0 0.0 collective-permute-done
  6.0 0.1 broadcast_select_fusion.4
  6.1 0.2 broadcast_select_fusion.1
  6.3 0.1 pad_maximum_fusion.2
  6.5 1.6 %collective-permute-start.1 = (bf16[4,88,96]{2,1,0:T(8,128)(2,1)S(1)}, bf16[4,88,96]{2,1,0:T(8,128)(2,1)S(1)}, u32[]{:S(2)}, u32[]{:S(2)}) collective-permute-start(bf16[4,88,96]{2,1,0:T(8,128)(2,1)S(1)} %pad_maximum_fusion.2), channel_id=1, source_target_pairs={{0,1},{1,0},{2,3},{3,2},{4,5},{5,4},{6,7},{7,6},{8,9},{9,8},{10,11... | collective-permute-start | bytes 202760 | tf_op jit(solution)/shard_map/ppermute | solution.py:209
  8.1 0.0 copy-done.1
  8.1 0.0 copy-done.4
  8.1 3.5 %collective-permute-done.1 = bf16[4,88,96]{2,1,0:T(8,128)(2,1)S(1)} collective-permute-done((bf16[4,88,96]{2,1,0:T(8,128)(2,1)S(1)}, bf16[4,88,96]{2,1,0:T(8,128)(2,1)S(1)}, u32[]{:S(2)}, u32[]{:S(2)}) %collective-permute-start.1) | collective-permute-done | bytes 67616 | tf_op jit(solution)/shard_map/ppermute | solution.py:209
  11.5 0.1 fusion.17
  11.7 0.2 broadcast_select_fusion.2
  11.9 0.3 fusion.12.own_ref
  12.2 0.1 fusion.14
  12.3 3.8 %collective-permute-start.2 = (bf16[12,80,128]{2,1,0:T(8,128)(2,1)S(1)}, bf16[12,80,128]{2,1,0:T(8,128)(2,1)S(1)}, u32[]{:S(2)}, u32[]{:S(2)}) collective-permute-start(bf16[12,80,128]{2,1,0:T(8,128)(2,1)S(1)} %get-tuple-element.50), channel_id=1, source_target_pairs={{0,4},{2,6},{4,8},{6,10},{8,12},{10,14},{12,16},{14,18},{16,20},{1... | collective-permute-start | bytes 737288 | tf_op jit(solution)/shard_map/ppermute | solution.py:182
  16.1 0.0 copy-start
  16.1 2.2 %collective-permute-start.3 = (bf16[12,80,128]{2,1,0:T(8,128)(2,1)S(1)}, bf16[12,80,128]{2,1,0:T(8,128)(2,1)S(1)}, u32[]{:S(2)}, u32[]{:S(2)}) collective-permute-start(bf16[12,80,128]{2,1,0:T(8,128)(2,1)S(1)} %get-tuple-element.49), channel_id=1, source_target_pairs={{4,0},{6,2},{8,4},{10,6},{12,8},{14,10},{16,12},{18,14},{20,16},{2... | collective-permute-start | bytes 737288 | tf_op jit(solution)/shard_map/ppermute | solution.py:182
  18.3 0.5 fusion.1.mix_ref
  18.8 2.8 %collective-permute-done.2.up_ref = bf16[12,80,128]{2,1,0:T(8,128)(2,1)S(1)} collective-permute-done((bf16[12,80,128]{2,1,0:T(8,128)(2,1)S(1)}, bf16[12,80,128]{2,1,0:T(8,128)(2,1)S(1)}, u32[]{:S(2)}, u32[]{:S(2)}) %collective-permute-start.2) | collective-permute-done | bytes 245792 | tf_op jit(solution)/shard_map/ppermute | solution.py:182
  21.6 3.9 %collective-permute-done.3.down_ref = bf16[12,80,128]{2,1,0:T(8,128)(2,1)S(1)} collective-permute-done((bf16[12,80,128]{2,1,0:T(8,128)(2,1)S(1)}, bf16[12,80,128]{2,1,0:T(8,128)(2,1)S(1)}, u32[]{:S(2)}, u32[]{:S(2)}) %collective-permute-start.3) | collective-permute-done | bytes 245792 | tf_op jit(solution)/shard_map/ppermute | solution.py:182
  25.5 0.1 broadcast_in_dim.4.taps_ref
  25.6 0.0 copy-done
  25.6 39.9 %rollout_step.2.own_ref = bf16[16,80,128]{2,1,0:T(8,128)(2,1)S(1)} custom-call(bf16[12,80,128]{2,1,0:T(8,128)(2,1)S(1)} %collective-permute-done.2.up_ref, bf16[16,88,128]{2,1,0:T(8,128)(2,1)S(1)} %fusion.12.own_ref, bf16[12,80,128]{2,1,0:T(8,128)(2,1)S(1)} %collective-permute-done.3.down_ref, bf16[80,512]{1,0:T(8,128)(2,1)S(1)} %maximum_bitcast_fusion.1.enc_ref, ...), custom_call_target="tpu_custom_call" | custom-call | tf_op jit(solution)/shard_map/rollout_step/pallas_call | solution.py:164
  65.5 0.1 fusion.16
  65.5 5.0 %collective-permute-start.4 = (bf16[12,80,128]{2,1,0:T(8,128)(2,1)S(1)}, bf16[12,80,128]{2,1,0:T(8,128)(2,1)S(1)}, u32[]{:S(2)}, u32[]{:S(2)}) collective-permute-start(bf16[12,80,128]{2,1,0:T(8,128)(2,1)S(1)} %get-tuple-element.58), channel_id=1, source_target_pairs={{0,4},{2,6},{4,8},{6,10},{8,12},{10,14},{12,16},{14,18},{16,20},{1... | collective-permute-start | bytes 737288 | tf_op jit(solution)/shard_map/ppermute | solution.py:182
  70.6 1.9 %collective-permute-start.5 = (bf16[12,80,128]{2,1,0:T(8,128)(2,1)S(1)}, bf16[12,80,128]{2,1,0:T(8,128)(2,1)S(1)}, u32[]{:S(2)}, u32[]{:S(2)}) collective-permute-start(bf16[12,80,128]{2,1,0:T(8,128)(2,1)S(1)} %get-tuple-element.57), channel_id=1, source_target_pairs={{4,0},{6,2},{8,4},{10,6},{12,8},{14,10},{16,12},{18,14},{20,16},{2... | collective-permute-start | bytes 737288 | tf_op jit(solution)/shard_map/ppermute | solution.py:182
  72.6 2.1 %collective-permute-done.4.up_ref = bf16[12,80,128]{2,1,0:T(8,128)(2,1)S(1)} collective-permute-done((bf16[12,80,128]{2,1,0:T(8,128)(2,1)S(1)}, bf16[12,80,128]{2,1,0:T(8,128)(2,1)S(1)}, u32[]{:S(2)}, u32[]{:S(2)}) %collective-permute-start.4) | collective-permute-done | bytes 245792 | tf_op jit(solution)/shard_map/ppermute | solution.py:182
  74.7 5.0 %collective-permute-done.5.down_ref = bf16[12,80,128]{2,1,0:T(8,128)(2,1)S(1)} collective-permute-done((bf16[12,80,128]{2,1,0:T(8,128)(2,1)S(1)}, bf16[12,80,128]{2,1,0:T(8,128)(2,1)S(1)}, u32[]{:S(2)}, u32[]{:S(2)}) %collective-permute-start.5) | collective-permute-done | bytes 245792 | tf_op jit(solution)/shard_map/ppermute | solution.py:182
  79.7 34.7 %rollout_step.3 = bf16[16,72,128]{2,1,0:T(8,128)(2,1)S(1)} custom-call(bf16[12,80,128]{2,1,0:T(8,128)(2,1)S(1)} %collective-permute-done.4.up_ref, bf16[16,80,128]{2,1,0:T(8,128)(2,1)S(1)} %rollout_step.2.own_ref, bf16[12,80,128]{2,1,0:T(8,128)(2,1)S(1)} %collective-permute-done.5.down_ref, bf16[80,512]{1,0:T(8,128)(2,1)S(1)} %maximum_bitcast_fusion.1.enc_ref, ...), custom_call_target="tpu_custom_call" | custom-call | tf_op jit(solution)/shard_map/rollout_step/pallas_call | solution.py:164
  114.4 0.1 broadcast_select_fusion.3
  114.5 0.1 collective-permute-start.6
  114.6 1.6 %collective-permute-done.6 = bf16[2,8,72,128]{3,2,1,0:T(8,128)(2,1)S(1)} collective-permute-done((bf16[2,8,72,128]{3,2,1,0:T(8,128)(2,1)S(1)}, bf16[2,8,72,128]{3,2,1,0:T(8,128)(2,1)S(1)}, u32[]{:S(2)}, u32[]{:S(2)}) %collective-permute-start.6) | collective-permute-done | bytes 294944 | tf_op jit(solution)/shard_map/ppermute | solution.py:239
  116.2 0.1 select_bitcast_fusion
  116.2 0.7 copy.45
  117.0 6.9 %all-to-all-start = ((bf16[1,2,72,8,128]{4,3,1,0,2:T(8,128)(2,1)}), bf16[1,2,72,8,128]{4,3,1,0,2:T(8,128)(2,1)S(1)}, u32[]{:S(2)}, u32[]{:S(2)}) async-start(bf16[1,2,72,8,128]{4,3,1,0,2:T(8,128)(2,1)} %copy.45), calls=%async_computation | async-start | bytes 589824 | tf_op jit(solution)/shard_map/all_to_all | solution.py:247
  123.9 0.8 dynamic-slice_convert_fusion
  124.7 0.8 copy.47
  125.4 7.8 %all-to-all-done = bf16[1,2,72,8,128]{4,3,1,0,2:T(8,128)(2,1)S(1)} async-done(((bf16[1,2,72,8,128]{4,3,1,0,2:T(8,128)(2,1)}), bf16[1,2,72,8,128]{4,3,1,0,2:T(8,128)(2,1)S(1)}, u32[]{:S(2)}, u32[]{:S(2)}) %all-to-all-start) | async-done | bytes 294944 | tf_op jit(solution)/shard_map/all_to_all | solution.py:247
  133.3 0.2 abs_reduce_fusion.26
  133.4 0.1 abs_reduce_fusion.25
  133.5 0.1 fusion.5
  133.6 0.7 multiply_subtract_fusion
  (14 shorter events, 0.2 us)
Async XLA Ops:
  2.3 3.7 %collective-permute-start = (bf16[8,88,128]{2,1,0:T(8,128)(2,1)S(1)}, bf16[8,88,128]{2,1,0:T(8,128)(2,1)S(1)}, u32[]{:S(2)}, u32[]{:S(2)}) collective-permute-start(bf16[8,88,128]{2,1,0:T(8,128)(2,1)S(1)} %maximum_bitcast_fusion), channel_id=1, source_target_pairs={{0,2},{2,0},{4,6},{6,4},{8,10},{10,8},{12,14},{14,12},{16,18},{18,... | collective-permute-start | bytes 540680 | tf_op jit(solution)/shard_map/ppermute | solution.py:200
  2.5 2.9 %copy-start.5 = (f32[4,512]{1,0:T(4,128)S(1)}, f32[4,512]{1,0:T(4,128)}, u32[]{:S(2)}) copy-start(f32[4,512]{1,0:T(4,128)} %param.17) | copy-start | bytes 24580
  2.5 2.9 %copy-start.2 = (f32[4,7,512]{2,0,1:T(4,128)S(1)}, f32[4,7,512]{2,0,1:T(4,128)}, u32[]{:S(2)}) copy-start(f32[4,7,512]{2,0,1:T(4,128)} %param.15) | copy-start | bytes 172036
  2.5 2.9 %copy-start.3 = (f32[4,6,512]{2,0,1:T(4,128)S(1)}, f32[4,6,512]{2,0,1:T(4,128)}, u32[]{:S(2)}) copy-start(f32[4,6,512]{2,0,1:T(4,128)} %param.16) | copy-start | bytes 147460
  5.5 2.6 %copy-start.1 = (bf16[512,72]{0,1:T(8,128)(2,1)S(1)}, bf16[512,72]{0,1:T(8,128)(2,1)}, u32[]{:S(2)}) copy-start(bf16[512,72]{0,1:T(8,128)(2,1)} %param.13) | copy-start | bytes 221188
  5.5 2.6 %copy-start.4 = (bf16[512,8]{0,1:T(8,128)(2,1)S(1)}, bf16[512,8]{0,1:T(8,128)(2,1)}, u32[]{:S(2)}) copy-start(bf16[512,8]{0,1:T(8,128)(2,1)} %param.14) | copy-start | bytes 24580
  6.5 5.1 %collective-permute-start.1 = (bf16[4,88,96]{2,1,0:T(8,128)(2,1)S(1)}, bf16[4,88,96]{2,1,0:T(8,128)(2,1)S(1)}, u32[]{:S(2)}, u32[]{:S(2)}) collective-permute-start(bf16[4,88,96]{2,1,0:T(8,128)(2,1)S(1)} %pad_maximum_fusion.2), channel_id=1, source_target_pairs={{0,1},{1,0},{2,3},{3,2},{4,5},{5,4},{6,7},{7,6},{8,9},{9,8},{10,11... | collective-permute-start | bytes 202760 | tf_op jit(solution)/shard_map/ppermute | solution.py:209
  12.3 9.3 %collective-permute-start.2 = (bf16[12,80,128]{2,1,0:T(8,128)(2,1)S(1)}, bf16[12,80,128]{2,1,0:T(8,128)(2,1)S(1)}, u32[]{:S(2)}, u32[]{:S(2)}) collective-permute-start(bf16[12,80,128]{2,1,0:T(8,128)(2,1)S(1)} %get-tuple-element.50), channel_id=1, source_target_pairs={{0,4},{2,6},{4,8},{6,10},{8,12},{10,14},{12,16},{14,18},{16,20},{1... | collective-permute-start | bytes 737288 | tf_op jit(solution)/shard_map/ppermute | solution.py:182
  16.1 9.5 %copy-start = (bf16[72,512]{1,0:T(8,128)(2,1)S(1)}, bf16[72,512]{1,0:T(8,128)(2,1)}, u32[]{:S(2)}) copy-start(bf16[72,512]{1,0:T(8,128)(2,1)} %dec_ref.3) | copy-start | bytes 221188
  16.1 9.4 %collective-permute-start.3 = (bf16[12,80,128]{2,1,0:T(8,128)(2,1)S(1)}, bf16[12,80,128]{2,1,0:T(8,128)(2,1)S(1)}, u32[]{:S(2)}, u32[]{:S(2)}) collective-permute-start(bf16[12,80,128]{2,1,0:T(8,128)(2,1)S(1)} %get-tuple-element.49), channel_id=1, source_target_pairs={{4,0},{6,2},{8,4},{10,6},{12,8},{14,10},{16,12},{18,14},{20,16},{2... | collective-permute-start | bytes 737288 | tf_op jit(solution)/shard_map/ppermute | solution.py:182
  65.5 9.1 %collective-permute-start.4 = (bf16[12,80,128]{2,1,0:T(8,128)(2,1)S(1)}, bf16[12,80,128]{2,1,0:T(8,128)(2,1)S(1)}, u32[]{:S(2)}, u32[]{:S(2)}) collective-permute-start(bf16[12,80,128]{2,1,0:T(8,128)(2,1)S(1)} %get-tuple-element.58), channel_id=1, source_target_pairs={{0,4},{2,6},{4,8},{6,10},{8,12},{10,14},{12,16},{14,18},{16,20},{1... | collective-permute-start | bytes 737288 | tf_op jit(solution)/shard_map/ppermute | solution.py:182
  70.6 9.1 %collective-permute-start.5 = (bf16[12,80,128]{2,1,0:T(8,128)(2,1)S(1)}, bf16[12,80,128]{2,1,0:T(8,128)(2,1)S(1)}, u32[]{:S(2)}, u32[]{:S(2)}) collective-permute-start(bf16[12,80,128]{2,1,0:T(8,128)(2,1)S(1)} %get-tuple-element.57), channel_id=1, source_target_pairs={{4,0},{6,2},{8,4},{10,6},{12,8},{14,10},{16,12},{18,14},{20,16},{2... | collective-permute-start | bytes 737288 | tf_op jit(solution)/shard_map/ppermute | solution.py:182
  114.5 1.7 %collective-permute-start.6 = (bf16[2,8,72,128]{3,2,1,0:T(8,128)(2,1)S(1)}, bf16[2,8,72,128]{3,2,1,0:T(8,128)(2,1)S(1)}, u32[]{:S(2)}, u32[]{:S(2)}) collective-permute-start(bf16[2,8,72,128]{3,2,1,0:T(8,128)(2,1)S(1)} %broadcast_select_fusion.3), channel_id=1, source_target_pairs={{0,2},{2,0},{4,6},{6,4},{8,10},{10,8},{12,14},{14,12},{16,18},{18,... | collective-permute-start | bytes 884744 | tf_op jit(solution)/shard_map/ppermute | solution.py:239
  117.0 16.3 %all-to-all-start = ((bf16[1,2,72,8,128]{4,3,1,0,2:T(8,128)(2,1)}), bf16[1,2,72,8,128]{4,3,1,0,2:T(8,128)(2,1)S(1)}, u32[]{:S(2)}, u32[]{:S(2)}) async-start(bf16[1,2,72,8,128]{4,3,1,0,2:T(8,128)(2,1)} %copy.45), calls=%async_computation | async-start | bytes 589824 | tf_op jit(solution)/shard_map/all_to_all | solution.py:247

commit v2 on v1

--- a/solution.py
+++ b/solution.py
@@ -27,6 +27,8 @@
     v_ref,
     acc_ref,
     scale_ref,
+    sum_ref,
+    square_ref,
 ):
     halo = up_ref.shape[0]
     own = own_ref.shape[0]
@@ -62,7 +64,7 @@
                     ]
             return 0
 
-        lax.fori_loop(0, source.shape[0], one, 0)
+        lax.fori_loop(0, source.shape[0], one, 0, unroll=4)
 
     encode(up_ref, 0)
     encode(own_ref, halo)
@@ -82,6 +84,8 @@
 
             def convolve(j, _):
                 c = pl.multiple_of(left + 16 * j, 8)
+                sums = [None] * 4
+                squares = [None] * 4
                 for t in range(planes):
                     part = slice(t * lanes, (t + 1) * lanes)
                     rows = [h_ref[t, k + i, pl.ds(c, 16), :].astype(BF16) for i in range(10)]
@@ -99,6 +103,13 @@
                     for r in range(4):
                         m = pl.multiple_of(r * 16 * tiles + 16 * j, 16)
                         v_ref[pl.ds(m, 16), part] = totals[r]
+                        square = totals[r] * totals[r]
+                        sums[r] = totals[r] if t == 0 else sums[r] + totals[r]
+                        squares[r] = square if t == 0 else squares[r] + square
+                for r in range(4):
+                    m = pl.multiple_of(r * 16 * tiles + 16 * j, 16)
+                    sum_ref[pl.ds(m, 16), :] = sums[r].astype(F32)
+                    square_ref[pl.ds(m, 16), :] = squares[r].astype(F32)
                 return 0
 
             lax.fori_loop(0, tiles, convolve, 0)
@@ -111,11 +122,8 @@
                 inside = jnp.logical_and(row >= 0, row < height).astype(F32)
                 for j in range(tiles):
                     m = r * 16 * tiles + 16 * j
-                    parts = [
-                        v_ref[m : m + 16, t * lanes : (t + 1) * lanes] for t in range(planes)
-                    ]
-                    total = functools.reduce(jnp.add, parts).astype(F32)
-                    square = functools.reduce(jnp.add, [x * x for x in parts]).astype(F32)
+                    total = sum_ref[m : m + 16, :]
+                    square = square_ref[m : m + 16, :]
                     mean = jnp.sum(total, axis=1, keepdims=True)
                     second = jnp.sum(square, axis=1, keepdims=True)
                     variance = jnp.maximum(
@@ -151,7 +159,7 @@
             out_ref[k, variables:] = own_ref[k, inputs:]
         return 0
 
-    lax.fori_loop(0, own, decode, 0)
+    lax.fori_loop(0, own, decode, 0, unroll=4)
 
 
 def rollout_step(up, own, down, enc, taps, mix, dec, width, carry_noise):
@@ -171,6 +179,8 @@
             pltpu.VMEM((cells, channels), BF16),
             pltpu.VMEM((cells, channels), F32),
             pltpu.VMEM((cells, lanes), F32),
+            pltpu.VMEM((cells, lanes), F32),
+            pltpu.VMEM((cells, lanes), F32),
         ],
         compiler_params=pltpu.CompilerParams(vmem_limit_bytes=48 * 1024 * 1024),
         name="rollout_step",
@@ -206,6 +216,7 @@
     left = block[:, :, :side]
     edge = jnp.where(core == 0, right, left).reshape(4, rows // 4, -1, side)
     packed = jnp.concatenate([edge[i] for i in range(4)], axis=-1)
+    mix, gains, _ = lax.optimization_barrier((mix, gains, packed))
     packed = lax.ppermute(packed, "lon", [(0, 1), (1, 0)])
     edge = jnp.concatenate([packed[:, :, i * side : (i + 1) * side] for i in range(4)], axis=0)
     block = jnp.concatenate(

time: 135 us -> 121 us (0.90)
  Pallas kernels: 74.6 us -> 61.6 us
  other arithmetic: 4.06 us -> 6.58 us
  waiting for transfers between devices: 26.6 us -> 24.2 us
    pallas_call x2, Pallas kernels: 74.6 us -> 61.6 us  [rollout_step(): pl.pallas_call(functools.partial(step_kernel, width), out_shape=jax.Shape...]
    ppermute x1, waiting for transfers between devices: 3.46 us -> 0.18 us  [local(): packed = lax.ppermute(packed, 'lon', [(0, 1), (1, 0)])]
    unnamed x15 -> x6, local copies, waits for them, and re-layouts: 4.54 us -> 1.7 us
    optimization_barrier x0 -> x1, local copies, waits for them, and re-layouts: none -> 2.79 us  [local(): mix, gains, _ = lax.optimization_barrier((mix, gains, packed))]
    another operation x2, other arithmetic: 0.02 us -> 1.64 us
  transfers between devices with their start and end apart: 8 -> 8, of which waited for: 7 -> 7; matrix products, arithmetic and copies ran while one was open for 4% -> 7% of each run, Pallas kernels for 0% -> 0%
where the time goes in v2:
time: 121 us
  Pallas kernels  61.6 us (51%)
  waiting for transfers between devices  24.2 us (20%)
  starting transfers between devices  21.1 us (17%)
  other arithmetic  6.58 us (5%)
  local copies, waits for them, and re-layouts  6.38 us (5%)
    pallas_call x2, Pallas kernels, rollout_step(): pl.pallas_call(functools.partial(step_kernel, width), out_shape=jax.Shape...  61.6 us
    ppermute x4, waiting for transfers between devices, z_shift(): return lax.ppermute(block, 'lat', pairs)  14.7 us
    ppermute x4, starting transfers between devices, z_shift(): return lax.ppermute(block, 'lat', pairs)  13 us
    all_to_all x1, waiting for transfers between devices, local(): lax.all_to_all(trajectory_predictions, 'member', split_axis=2, concat_axi...  7.8 us
    all_to_all x1, starting transfers between devices, local(): lax.all_to_all(trajectory_predictions, 'member', split_axis=2, concat_axi...  6.35 us
    optimization_barrier x1, local copies, waits for them, and re-layouts, local(): mix, gains, _ = lax.optimization_barrier((mix, gains, packed))  2.79 us
  transfers between devices with their start and end apart: 8, of which 7 were waited for; matrix products, arithmetic and copies ran while one was open for 7% of the time, Pallas kernels for 0%

profile of v2, /device:TPU:32, one launch (start us, length us, event | category | flops | bytes accessed | tf_op | source)
XLA Modules:
  0.0 120.7 jit_solution(12704095777608629949)
XLA Ops:
  0.6 0.7 fusion.18
  1.4 0.9 copy.42
  2.3 0.1 collective-permute-start
  2.5 0.8 convert.8
  3.3 0.8 convert.9
  4.2 0.9 maximum_bitcast_fusion.1.enc_ref
  5.1 0.0 collective-permute-done
  5.1 0.1 broadcast_select_fusion.4
  5.2 0.2 broadcast_select_fusion.1
  5.4 0.1 pad_maximum_fusion.2
  5.5 0.0 copy-start.1
  5.6 1.6 %collective-permute-start.1 = (bf16[4,88,96]{2,1,0:T(8,128)(2,1)S(1)}, bf16[4,88,96]{2,1,0:T(8,128)(2,1)S(1)}, u32[]{:S(2)}, u32[]{:S(2)}) collective-permute-start(bf16[4,88,96]{2,1,0:T(8,128)(2,1)S(1)} %pad_maximum_fusion.2), channel_id=1, source_target_pairs={{0,1},{1,0},{2,3},{3,2},{4,5},{5,4},{6,7},{7,6},{8,9},{9,8},{10,11... | collective-permute-start | bytes 202760 | tf_op jit(solution)/shard_map/ppermute | solution.py:220
  7.1 2.8 %copy.44 = bf16[4,512,512]{1,2,0:T(8,128)(2,1)S(1)} copy(bf16[4,512,512]{2,1,0:T(8,128)(2,1)} %param.18) | data formatting | bytes 4194304 | tf_op jit(solution)/shard_map/optimization_barrier | solution.py:219
  9.9 0.0 copy-done.1
  10.0 0.5 fusion
  10.5 0.2 collective-permute-done.1
  10.6 0.1 fusion.17
  10.8 0.2 broadcast_select_fusion.2
  11.0 0.3 fusion.12.own_ref
  11.3 0.1 fusion.14
  11.4 3.8 %collective-permute-start.2 = (bf16[12,80,128]{2,1,0:T(8,128)(2,1)S(1)}, bf16[12,80,128]{2,1,0:T(8,128)(2,1)S(1)}, u32[]{:S(2)}, u32[]{:S(2)}) collective-permute-start(bf16[12,80,128]{2,1,0:T(8,128)(2,1)S(1)} %get-tuple-element.54), channel_id=1, source_target_pairs={{0,4},{2,6},{4,8},{6,10},{8,12},{10,14},{12,16},{14,18},{16,20},{1... | collective-permute-start | bytes 737288 | tf_op jit(solution)/shard_map/ppermute | solution.py:192
  15.2 0.0 copy-start
  15.2 2.2 %collective-permute-start.3 = (bf16[12,80,128]{2,1,0:T(8,128)(2,1)S(1)}, bf16[12,80,128]{2,1,0:T(8,128)(2,1)S(1)}, u32[]{:S(2)}, u32[]{:S(2)}) collective-permute-start(bf16[12,80,128]{2,1,0:T(8,128)(2,1)S(1)} %get-tuple-element.53), channel_id=1, source_target_pairs={{4,0},{6,2},{8,4},{10,6},{12,8},{14,10},{16,12},{18,14},{20,16},{2... | collective-permute-start | bytes 737288 | tf_op jit(solution)/shard_map/ppermute | solution.py:192
  17.4 0.6 fusion.1.mix_ref
  18.0 3.2 %collective-permute-done.2.up_ref = bf16[12,80,128]{2,1,0:T(8,128)(2,1)S(1)} collective-permute-done((bf16[12,80,128]{2,1,0:T(8,128)(2,1)S(1)}, bf16[12,80,128]{2,1,0:T(8,128)(2,1)S(1)}, u32[]{:S(2)}, u32[]{:S(2)}) %collective-permute-start.2) | collective-permute-done | bytes 245792 | tf_op jit(solution)/shard_map/ppermute | solution.py:192
  21.2 3.9 %collective-permute-done.3.down_ref = bf16[12,80,128]{2,1,0:T(8,128)(2,1)S(1)} collective-permute-done((bf16[12,80,128]{2,1,0:T(8,128)(2,1)S(1)}, bf16[12,80,128]{2,1,0:T(8,128)(2,1)S(1)}, u32[]{:S(2)}, u32[]{:S(2)}) %collective-permute-start.3) | collective-permute-done | bytes 245792 | tf_op jit(solution)/shard_map/ppermute | solution.py:192
  25.1 0.1 broadcast_in_dim.4.taps_ref
  25.1 0.0 copy-done
  25.1 33.6 %rollout_step.2.own_ref = bf16[16,80,128]{2,1,0:T(8,128)(2,1)S(1)} custom-call(bf16[12,80,128]{2,1,0:T(8,128)(2,1)S(1)} %collective-permute-done.2.up_ref, bf16[16,88,128]{2,1,0:T(8,128)(2,1)S(1)} %fusion.12.own_ref, bf16[12,80,128]{2,1,0:T(8,128)(2,1)S(1)} %collective-permute-done.3.down_ref, bf16[80,512]{1,0:T(8,128)(2,1)S(1)} %maximum_bitcast_fusion.1.enc_ref, ...), custom_call_target="tpu_custom_call" | custom-call | tf_op jit(solution)/shard_map/rollout_step/pallas_call | solution.py:172
  58.8 0.1 fusion.16
  58.8 5.1 %collective-permute-start.4 = (bf16[12,80,128]{2,1,0:T(8,128)(2,1)S(1)}, bf16[12,80,128]{2,1,0:T(8,128)(2,1)S(1)}, u32[]{:S(2)}, u32[]{:S(2)}) collective-permute-start(bf16[12,80,128]{2,1,0:T(8,128)(2,1)S(1)} %get-tuple-element.62), channel_id=1, source_target_pairs={{0,4},{2,6},{4,8},{6,10},{8,12},{10,14},{12,16},{14,18},{16,20},{1... | collective-permute-start | bytes 737288 | tf_op jit(solution)/shard_map/ppermute | solution.py:192
  63.9 1.9 %collective-permute-start.5 = (bf16[12,80,128]{2,1,0:T(8,128)(2,1)S(1)}, bf16[12,80,128]{2,1,0:T(8,128)(2,1)S(1)}, u32[]{:S(2)}, u32[]{:S(2)}) collective-permute-start(bf16[12,80,128]{2,1,0:T(8,128)(2,1)S(1)} %get-tuple-element.61), channel_id=1, source_target_pairs={{4,0},{6,2},{8,4},{10,6},{12,8},{14,10},{16,12},{18,14},{20,16},{2... | collective-permute-start | bytes 737288 | tf_op jit(solution)/shard_map/ppermute | solution.py:192
  65.9 2.5 %collective-permute-done.4.up_ref = bf16[12,80,128]{2,1,0:T(8,128)(2,1)S(1)} collective-permute-done((bf16[12,80,128]{2,1,0:T(8,128)(2,1)S(1)}, bf16[12,80,128]{2,1,0:T(8,128)(2,1)S(1)}, u32[]{:S(2)}, u32[]{:S(2)}) %collective-permute-start.4) | collective-permute-done | bytes 245792 | tf_op jit(solution)/shard_map/ppermute | solution.py:192
  68.4 5.0 %collective-permute-done.5.down_ref = bf16[12,80,128]{2,1,0:T(8,128)(2,1)S(1)} collective-permute-done((bf16[12,80,128]{2,1,0:T(8,128)(2,1)S(1)}, bf16[12,80,128]{2,1,0:T(8,128)(2,1)S(1)}, u32[]{:S(2)}, u32[]{:S(2)}) %collective-permute-start.5) | collective-permute-done | bytes 245792 | tf_op jit(solution)/shard_map/ppermute | solution.py:192
  73.4 28.0 %rollout_step.3 = bf16[16,72,128]{2,1,0:T(8,128)(2,1)S(1)} custom-call(bf16[12,80,128]{2,1,0:T(8,128)(2,1)S(1)} %collective-permute-done.4.up_ref, bf16[16,80,128]{2,1,0:T(8,128)(2,1)S(1)} %rollout_step.2.own_ref, bf16[12,80,128]{2,1,0:T(8,128)(2,1)S(1)} %collective-permute-done.5.down_ref, bf16[80,512]{1,0:T(8,128)(2,1)S(1)} %maximum_bitcast_fusion.1.enc_ref, ...), custom_call_target="tpu_custom_call" | custom-call | tf_op jit(solution)/shard_map/rollout_step/pallas_call | solution.py:172
  101.4 0.1 broadcast_select_fusion.3
  101.5 0.1 collective-permute-start.6
  101.6 1.6 %collective-permute-done.6 = bf16[2,8,72,128]{3,2,1,0:T(8,128)(2,1)S(1)} collective-permute-done((bf16[2,8,72,128]{3,2,1,0:T(8,128)(2,1)S(1)}, bf16[2,8,72,128]{3,2,1,0:T(8,128)(2,1)S(1)}, u32[]{:S(2)}, u32[]{:S(2)}) %collective-permute-start.6) | collective-permute-done | bytes 294944 | tf_op jit(solution)/shard_map/ppermute | solution.py:250
  103.1 0.1 select_bitcast_fusion
  103.2 0.7 copy.45
  103.9 6.3 %all-to-all-start = ((bf16[1,2,72,8,128]{4,3,1,0,2:T(8,128)(2,1)}), bf16[1,2,72,8,128]{4,3,1,0,2:T(8,128)(2,1)S(1)}, u32[]{:S(2)}, u32[]{:S(2)}) async-start(bf16[1,2,72,8,128]{4,3,1,0,2:T(8,128)(2,1)} %copy.45), calls=%async_computation | async-start | bytes 589824 | tf_op jit(solution)/shard_map/all_to_all | solution.py:258
  110.3 0.8 dynamic-slice_convert_fusion
  111.1 0.8 copy.47
  111.8 7.8 %all-to-all-done = bf16[1,2,72,8,128]{4,3,1,0,2:T(8,128)(2,1)S(1)} async-done(((bf16[1,2,72,8,128]{4,3,1,0,2:T(8,128)(2,1)}), bf16[1,2,72,8,128]{4,3,1,0,2:T(8,128)(2,1)S(1)}, u32[]{:S(2)}, u32[]{:S(2)}) %all-to-all-start) | async-done | bytes 294944 | tf_op jit(solution)/shard_map/all_to_all | solution.py:258
  119.7 0.2 abs_reduce_fusion.26
  119.8 0.1 abs_reduce_fusion.25
  119.9 0.1 fusion.5
  120.0 0.7 multiply_subtract_fusion
  (11 shorter events, 0.2 us)
Async XLA Ops:
  2.3 2.8 %collective-permute-start = (bf16[8,88,128]{2,1,0:T(8,128)(2,1)S(1)}, bf16[8,88,128]{2,1,0:T(8,128)(2,1)S(1)}, u32[]{:S(2)}, u32[]{:S(2)}) collective-permute-start(bf16[8,88,128]{2,1,0:T(8,128)(2,1)S(1)} %maximum_bitcast_fusion), channel_id=1, source_target_pairs={{0,2},{2,0},{4,6},{6,4},{8,10},{10,8},{12,14},{14,12},{16,18},{18,... | collective-permute-start | bytes 540680 | tf_op jit(solution)/shard_map/ppermute | solution.py:210
  5.5 4.4 %copy-start.1 = (f32[4,512]{1,0:T(4,128)S(1)}, f32[4,512]{1,0:T(4,128)}, u32[]{:S(2)}) copy-start(f32[4,512]{1,0:T(4,128)} %param.17) | copy-start | bytes 24580
  5.6 5.1 %collective-permute-start.1 = (bf16[4,88,96]{2,1,0:T(8,128)(2,1)S(1)}, bf16[4,88,96]{2,1,0:T(8,128)(2,1)S(1)}, u32[]{:S(2)}, u32[]{:S(2)}) collective-permute-start(bf16[4,88,96]{2,1,0:T(8,128)(2,1)S(1)} %pad_maximum_fusion.2), channel_id=1, source_target_pairs={{0,1},{1,0},{2,3},{3,2},{4,5},{5,4},{6,7},{7,6},{8,9},{9,8},{10,11... | collective-permute-start | bytes 202760 | tf_op jit(solution)/shard_map/ppermute | solution.py:220
  11.4 9.8 %collective-permute-start.2 = (bf16[12,80,128]{2,1,0:T(8,128)(2,1)S(1)}, bf16[12,80,128]{2,1,0:T(8,128)(2,1)S(1)}, u32[]{:S(2)}, u32[]{:S(2)}) collective-permute-start(bf16[12,80,128]{2,1,0:T(8,128)(2,1)S(1)} %get-tuple-element.54), channel_id=1, source_target_pairs={{0,4},{2,6},{4,8},{6,10},{8,12},{10,14},{12,16},{14,18},{16,20},{1... | collective-permute-start | bytes 737288 | tf_op jit(solution)/shard_map/ppermute | solution.py:192
  15.2 9.9 %copy-start = (bf16[72,512]{1,0:T(8,128)(2,1)S(1)}, bf16[72,512]{1,0:T(8,128)(2,1)}, u32[]{:S(2)}) copy-start(bf16[72,512]{1,0:T(8,128)(2,1)} %dec_ref.3) | copy-start | bytes 221188
  15.2 9.8 %collective-permute-start.3 = (bf16[12,80,128]{2,1,0:T(8,128)(2,1)S(1)}, bf16[12,80,128]{2,1,0:T(8,128)(2,1)S(1)}, u32[]{:S(2)}, u32[]{:S(2)}) collective-permute-start(bf16[12,80,128]{2,1,0:T(8,128)(2,1)S(1)} %get-tuple-element.53), channel_id=1, source_target_pairs={{4,0},{6,2},{8,4},{10,6},{12,8},{14,10},{16,12},{18,14},{20,16},{2... | collective-permute-start | bytes 737288 | tf_op jit(solution)/shard_map/ppermute | solution.py:192
  58.8 9.6 %collective-permute-start.4 = (bf16[12,80,128]{2,1,0:T(8,128)(2,1)S(1)}, bf16[12,80,128]{2,1,0:T(8,128)(2,1)S(1)}, u32[]{:S(2)}, u32[]{:S(2)}) collective-permute-start(bf16[12,80,128]{2,1,0:T(8,128)(2,1)S(1)} %get-tuple-element.62), channel_id=1, source_target_pairs={{0,4},{2,6},{4,8},{6,10},{8,12},{10,14},{12,16},{14,18},{16,20},{1... | collective-permute-start | bytes 737288 | tf_op jit(solution)/shard_map/ppermute | solution.py:192
  63.9 9.5 %collective-permute-start.5 = (bf16[12,80,128]{2,1,0:T(8,128)(2,1)S(1)}, bf16[12,80,128]{2,1,0:T(8,128)(2,1)S(1)}, u32[]{:S(2)}, u32[]{:S(2)}) collective-permute-start(bf16[12,80,128]{2,1,0:T(8,128)(2,1)S(1)} %get-tuple-element.61), channel_id=1, source_target_pairs={{4,0},{6,2},{8,4},{10,6},{12,8},{14,10},{16,12},{18,14},{20,16},{2... | collective-permute-start | bytes 737288 | tf_op jit(solution)/shard_map/ppermute | solution.py:192
  101.5 1.7 %collective-permute-start.6 = (bf16[2,8,72,128]{3,2,1,0:T(8,128)(2,1)S(1)}, bf16[2,8,72,128]{3,2,1,0:T(8,128)(2,1)S(1)}, u32[]{:S(2)}, u32[]{:S(2)}) collective-permute-start(bf16[2,8,72,128]{3,2,1,0:T(8,128)(2,1)S(1)} %broadcast_select_fusion.3), channel_id=1, source_target_pairs={{0,2},{2,0},{4,6},{6,4},{8,10},{10,8},{12,14},{14,12},{16,18},{18,... | collective-permute-start | bytes 884744 | tf_op jit(solution)/shard_map/ppermute | solution.py:250
  103.9 15.7 %all-to-all-start = ((bf16[1,2,72,8,128]{4,3,1,0,2:T(8,128)(2,1)}), bf16[1,2,72,8,128]{4,3,1,0,2:T(8,128)(2,1)S(1)}, u32[]{:S(2)}, u32[]{:S(2)}) async-start(bf16[1,2,72,8,128]{4,3,1,0,2:T(8,128)(2,1)} %copy.45), calls=%async_computation | async-start | bytes 589824 | tf_op jit(solution)/shard_map/all_to_all | solution.py:258

commit v3 on v2

--- a/solution.py
+++ b/solution.py
@@ -77,47 +77,47 @@
         edge = REACH * (level + 1)
         left = (inset + edge) // 8 * 8
         tiles = -(-(inset + width - edge - left) // 16)
-        groups = -(-(own + 2 * halo - 2 * edge) // 4)
-
-        def group(g, _, level=level, edge=edge, tiles=tiles, left=left + 8):
+        out_rows = own + 2 * halo - 2 * edge
+
+        def group(g, _, level=level, edge=edge, tiles=tiles, left=left + 8, deep=4):
             k = 4 * g
 
             def convolve(j, _):
                 c = pl.multiple_of(left + 16 * j, 8)
-                sums = [None] * 4
-                squares = [None] * 4
+                sums = [None] * deep
+                squares = [None] * deep
                 for t in range(planes):
                     part = slice(t * lanes, (t + 1) * lanes)
-                    rows = [h_ref[t, k + i, pl.ds(c, 16), :].astype(BF16) for i in range(10)]
-                    totals = [None] * 4
+                    rows = [h_ref[t, k + i, pl.ds(c, 16), :].astype(BF16) for i in range(deep + 6)]
+                    totals = [None] * deep
                     for d in range(7):
                         tap = taps_ref[level, d, :, part]
-                        for r in range(4):
+                        for r in range(deep):
                             term = rows[r + d] * tap
                             totals[r] = term if d == 0 else totals[r] + term
                     for column, d in enumerate([-3, -2, -1, 1, 2, 3]):
                         tap = taps_ref[level, 7 + column, :, part]
-                        for r in range(4):
+                        for r in range(deep):
                             shifted = h_ref[t, k + r + REACH, pl.ds(c + d, 16), :].astype(BF16)
                             totals[r] = totals[r] + shifted * tap
-                    for r in range(4):
+                    for r in range(deep):
                         m = pl.multiple_of(r * 16 * tiles + 16 * j, 16)
                         v_ref[pl.ds(m, 16), part] = totals[r]
                         square = totals[r] * totals[r]
                         sums[r] = totals[r] if t == 0 else sums[r] + totals[r]
                         squares[r] = square if t == 0 else squares[r] + square
-                for r in range(4):
+                for r in range(deep):
                     m = pl.multiple_of(r * 16 * tiles + 16 * j, 16)
                     sum_ref[pl.ds(m, 16), :] = sums[r].astype(F32)
                     square_ref[pl.ds(m, 16), :] = squares[r].astype(F32)
                 return 0
 
             lax.fori_loop(0, tiles, convolve, 0)
-            size = 64 * tiles
+            size = deep * 16 * tiles
             acc_ref[:size] = jnp.dot(
                 v_ref[:size], mix_ref[level], preferred_element_type=F32
             )
-            for r in range(4):
+            for r in range(deep):
                 row = first + edge + k + r
                 inside = jnp.logical_and(row >= 0, row < height).astype(F32)
                 for j in range(tiles):
@@ -133,7 +133,7 @@
                     scale_ref[m : m + 16, :] = jnp.broadcast_to(scale, (16, lanes))
             for j in range(tiles):
                 c = left + 16 * j
-                for r in range(4):
+                for r in range(deep):
                     m = r * 16 * tiles + 16 * j
                     scale = scale_ref[m : m + 16, :].astype(BF16)
                     for t in range(planes):
@@ -146,7 +146,9 @@
                         ] + gate.astype(F32)
             return 0
 
-        lax.fori_loop(0, groups, group, 0)
+        lax.fori_loop(0, out_rows // 4, group, 0)
+        if out_rows % 4:
+            group(out_rows // 4, 0, deep=out_rows % 4)
 
     def decode(k, _):
         h = jnp.concatenate([h_ref[t, k, pl.ds(8, span), :] for t in range(planes)], axis=1).astype(BF16)
@@ -230,6 +232,9 @@
     up = z_shift(block[rows - halo :, :inputs], 2, bands)
     down = z_shift(block[:halo, :inputs], -2, bands)
 
+    encoder_state_weight, enc_noise, lat_taps, lon_taps, _ = lax.optimization_barrier(
+        (encoder_state_weight, enc_noise, lat_taps, lon_taps, up)
+    )
     enc = jnp.concatenate([encoder_state_weight, enc_noise], axis=1).T
     taps = jnp.concatenate([lat_taps, lon_taps], axis=1).astype(BF16)
     taps = jnp.broadcast_to(taps[:, :, None, :], taps.shape[:2] + (16, channels))

time: 121 us -> 118 us (0.975)
  other arithmetic: 6.58 us -> 4.06 us
  Pallas kernels: 61.6 us -> 60.3 us
    another operation x2, other arithmetic: 1.64 us -> 0.02 us
    ppermute x1, waiting for transfers between devices: 0.01 us -> 1.39 us  [local(): other = lax.ppermute(mine, 'lat', sibling)]
    pallas_call x2, Pallas kernels: 61.6 us -> 60.3 us  [rollout_step(): pl.pallas_call(functools.partial(step_kernel, width), out_shape=jax.Shape...]
  transfers between devices with their start and end apart: 8 -> 8, of which waited for: 7 -> 7; matrix products, arithmetic and copies ran while one was open for 7% -> 5% of each run, Pallas kernels for 0% -> 0%
where the time goes in v3:
time: 118 us
  Pallas kernels  60.3 us (51%)
  waiting for transfers between devices  25 us (21%)
  starting transfers between devices  21.2 us (18%)
  local copies, waits for them, and re-layouts  6.41 us (5%)
  other arithmetic  4.06 us (3%)
    pallas_call x2, Pallas kernels, rollout_step(): pl.pallas_call(functools.partial(step_kernel, width), out_shape=jax.Shape...  60.3 us
    ppermute x4, waiting for transfers between devices, z_shift(): return lax.ppermute(block, 'lat', pairs)  14.2 us
    ppermute x4, starting transfers between devices, z_shift(): return lax.ppermute(block, 'lat', pairs)  12.9 us
    all_to_all x1, waiting for transfers between devices, local(): lax.all_to_all(trajectory_predictions, 'member', split_axis=2, concat_axi...  7.8 us
    all_to_all x1, starting transfers between devices, local(): lax.all_to_all(trajectory_predictions, 'member', split_axis=2, concat_axi...  6.51 us
    optimization_barrier x1, local copies, waits for them, and re-layouts, local(): mix, gains, _ = lax.optimization_barrier((mix, gains, packed))  2.79 us
  transfers between devices with their start and end apart: 8, of which 7 were waited for; matrix products, arithmetic and copies ran while one was open for 5% of the time, Pallas kernels for 0%

profile of v3, /device:TPU:32, one launch (start us, length us, event | category | flops | bytes accessed | tf_op | source)
XLA Modules:
  0.0 117.9 jit_solution(6956643281542828832)
XLA Ops:
  0.6 0.7 fusion.18
  1.4 0.9 copy.42
  2.3 0.1 collective-permute-start
  2.5 1.4 %collective-permute-done = bf16[8,88,128]{2,1,0:T(8,128)(2,1)S(1)} collective-permute-done((bf16[8,88,128]{2,1,0:T(8,128)(2,1)S(1)}, bf16[8,88,128]{2,1,0:T(8,128)(2,1)S(1)}, u32[]{:S(2)}, u32[]{:S(2)}) %collective-permute-start) | collective-permute-done | bytes 180256 | tf_op jit(solution)/shard_map/ppermute | solution.py:212
  3.9 0.1 broadcast_select_fusion.4
  3.9 0.2 broadcast_select_fusion.1
  4.1 0.1 pad_maximum_fusion.2
  4.3 0.0 copy-start.5
  4.3 1.6 %collective-permute-start.1 = (bf16[4,88,96]{2,1,0:T(8,128)(2,1)S(1)}, bf16[4,88,96]{2,1,0:T(8,128)(2,1)S(1)}, u32[]{:S(2)}, u32[]{:S(2)}) collective-permute-start(bf16[4,88,96]{2,1,0:T(8,128)(2,1)S(1)} %pad_maximum_fusion.2), channel_id=1, source_target_pairs={{0,1},{1,0},{2,3},{3,2},{4,5},{5,4},{6,7},{7,6},{8,9},{9,8},{10,11... | collective-permute-start | bytes 202760 | tf_op jit(solution)/shard_map/ppermute | solution.py:222
  5.9 2.8 %copy.44 = bf16[4,512,512]{1,2,0:T(8,128)(2,1)S(1)} copy(bf16[4,512,512]{2,1,0:T(8,128)(2,1)} %param.18) | data formatting | bytes 4194304 | tf_op jit(solution)/shard_map/optimization_barrier | solution.py:221
  8.7 0.0 copy-done.5
  8.7 0.5 fusion
  9.2 0.0 collective-permute-done.1
  9.2 0.1 fusion.17
  9.4 0.2 broadcast_select_fusion.2
  9.6 0.3 fusion.12.own_ref
  9.9 0.1 fusion.14
  10.0 3.8 %collective-permute-start.2 = (bf16[12,80,128]{2,1,0:T(8,128)(2,1)S(1)}, bf16[12,80,128]{2,1,0:T(8,128)(2,1)S(1)}, u32[]{:S(2)}, u32[]{:S(2)}) collective-permute-start(bf16[12,80,128]{2,1,0:T(8,128)(2,1)S(1)} %get-tuple-element.62), channel_id=1, source_target_pairs={{0,4},{2,6},{4,8},{6,10},{8,12},{10,14},{12,16},{14,18},{16,20},{1... | collective-permute-start | bytes 737288 | tf_op jit(solution)/shard_map/ppermute | solution.py:194
  13.8 0.0 copy-start.2
  13.8 0.0 copy-start.3
  13.8 0.0 copy-start.1
  13.8 0.0 copy-start.4
  13.9 0.0 copy-start
  13.9 2.2 %collective-permute-start.3 = (bf16[12,80,128]{2,1,0:T(8,128)(2,1)S(1)}, bf16[12,80,128]{2,1,0:T(8,128)(2,1)S(1)}, u32[]{:S(2)}, u32[]{:S(2)}) collective-permute-start(bf16[12,80,128]{2,1,0:T(8,128)(2,1)S(1)} %get-tuple-element.61), channel_id=1, source_target_pairs={{4,0},{6,2},{8,4},{10,6},{12,8},{14,10},{16,12},{18,14},{20,16},{2... | collective-permute-start | bytes 737288 | tf_op jit(solution)/shard_map/ppermute | solution.py:194
  16.0 0.6 fusion.1.mix_ref
  16.6 3.0 %collective-permute-done.2.up_ref = bf16[12,80,128]{2,1,0:T(8,128)(2,1)S(1)} collective-permute-done((bf16[12,80,128]{2,1,0:T(8,128)(2,1)S(1)}, bf16[12,80,128]{2,1,0:T(8,128)(2,1)S(1)}, u32[]{:S(2)}, u32[]{:S(2)}) %collective-permute-start.2) | collective-permute-done | bytes 245792 | tf_op jit(solution)/shard_map/ppermute | solution.py:194
  19.6 0.0 copy-done.2
  19.6 0.0 copy-done.3
  19.7 0.0 copy-done.1
  19.7 0.0 copy-done.4
  19.7 3.8 %collective-permute-done.3.down_ref = bf16[12,80,128]{2,1,0:T(8,128)(2,1)S(1)} collective-permute-done((bf16[12,80,128]{2,1,0:T(8,128)(2,1)S(1)}, bf16[12,80,128]{2,1,0:T(8,128)(2,1)S(1)}, u32[]{:S(2)}, u32[]{:S(2)}) %collective-permute-start.3) | collective-permute-done | bytes 245792 | tf_op jit(solution)/shard_map/ppermute | solution.py:194
  23.5 0.1 broadcast_in_dim.4.taps_ref
  23.6 0.0 copy-done
  23.6 32.9 %rollout_step.2.own_ref = bf16[16,80,128]{2,1,0:T(8,128)(2,1)S(1)} custom-call(bf16[12,80,128]{2,1,0:T(8,128)(2,1)S(1)} %collective-permute-done.2.up_ref, bf16[16,88,128]{2,1,0:T(8,128)(2,1)S(1)} %fusion.12.own_ref, bf16[12,80,128]{2,1,0:T(8,128)(2,1)S(1)} %collective-permute-done.3.down_ref, bf16[80,512]{1,0:T(8,128)(2,1)S(1)} %maximum_bitcast_fusion.1.enc_ref, ...), custom_call_target="tpu_custom_call" | custom-call | tf_op jit(solution)/shard_map/rollout_step/pallas_call | solution.py:174
  56.5 0.1 fusion.16
  56.6 5.0 %collective-permute-start.4 = (bf16[12,80,128]{2,1,0:T(8,128)(2,1)S(1)}, bf16[12,80,128]{2,1,0:T(8,128)(2,1)S(1)}, u32[]{:S(2)}, u32[]{:S(2)}) collective-permute-start(bf16[12,80,128]{2,1,0:T(8,128)(2,1)S(1)} %get-tuple-element.70), channel_id=1, source_target_pairs={{0,4},{2,6},{4,8},{6,10},{8,12},{10,14},{12,16},{14,18},{16,20},{1... | collective-permute-start | bytes 737288 | tf_op jit(solution)/shard_map/ppermute | solution.py:194
  61.6 1.9 %collective-permute-start.5 = (bf16[12,80,128]{2,1,0:T(8,128)(2,1)S(1)}, bf16[12,80,128]{2,1,0:T(8,128)(2,1)S(1)}, u32[]{:S(2)}, u32[]{:S(2)}) collective-permute-start(bf16[12,80,128]{2,1,0:T(8,128)(2,1)S(1)} %get-tuple-element.69), channel_id=1, source_target_pairs={{4,0},{6,2},{8,4},{10,6},{12,8},{14,10},{16,12},{18,14},{20,16},{2... | collective-permute-start | bytes 737288 | tf_op jit(solution)/shard_map/ppermute | solution.py:194
  63.6 2.4 %collective-permute-done.4.up_ref = bf16[12,80,128]{2,1,0:T(8,128)(2,1)S(1)} collective-permute-done((bf16[12,80,128]{2,1,0:T(8,128)(2,1)S(1)}, bf16[12,80,128]{2,1,0:T(8,128)(2,1)S(1)}, u32[]{:S(2)}, u32[]{:S(2)}) %collective-permute-start.4) | collective-permute-done | bytes 245792 | tf_op jit(solution)/shard_map/ppermute | solution.py:194
  66.0 5.0 %collective-permute-done.5.down_ref = bf16[12,80,128]{2,1,0:T(8,128)(2,1)S(1)} collective-permute-done((bf16[12,80,128]{2,1,0:T(8,128)(2,1)S(1)}, bf16[12,80,128]{2,1,0:T(8,128)(2,1)S(1)}, u32[]{:S(2)}, u32[]{:S(2)}) %collective-permute-start.5) | collective-permute-done | bytes 245792 | tf_op jit(solution)/shard_map/ppermute | solution.py:194
  71.0 27.4 %rollout_step.3 = bf16[16,72,128]{2,1,0:T(8,128)(2,1)S(1)} custom-call(bf16[12,80,128]{2,1,0:T(8,128)(2,1)S(1)} %collective-permute-done.4.up_ref, bf16[16,80,128]{2,1,0:T(8,128)(2,1)S(1)} %rollout_step.2.own_ref, bf16[12,80,128]{2,1,0:T(8,128)(2,1)S(1)} %collective-permute-done.5.down_ref, bf16[80,512]{1,0:T(8,128)(2,1)S(1)} %maximum_bitcast_fusion.1.enc_ref, ...), custom_call_target="tpu_custom_call" | custom-call | tf_op jit(solution)/shard_map/rollout_step/pallas_call | solution.py:174
  98.4 0.1 broadcast_select_fusion.3
  98.5 0.1 collective-permute-start.6
  98.6 1.6 %collective-permute-done.6 = bf16[2,8,72,128]{3,2,1,0:T(8,128)(2,1)S(1)} collective-permute-done((bf16[2,8,72,128]{3,2,1,0:T(8,128)(2,1)S(1)}, bf16[2,8,72,128]{3,2,1,0:T(8,128)(2,1)S(1)}, u32[]{:S(2)}, u32[]{:S(2)}) %collective-permute-start.6) | collective-permute-done | bytes 294944 | tf_op jit(solution)/shard_map/ppermute | solution.py:255
  100.1 0.1 select_bitcast_fusion
  100.2 0.7 copy.45
  101.0 6.5 %all-to-all-start = ((bf16[1,2,72,8,128]{4,3,1,0,2:T(8,128)(2,1)}), bf16[1,2,72,8,128]{4,3,1,0,2:T(8,128)(2,1)S(1)}, u32[]{:S(2)}, u32[]{:S(2)}) async-start(bf16[1,2,72,8,128]{4,3,1,0,2:T(8,128)(2,1)} %copy.45), calls=%async_computation | async-start | bytes 589824 | tf_op jit(solution)/shard_map/all_to_all | solution.py:263
  107.5 0.8 dynamic-slice_convert_fusion
  108.2 0.8 copy.47
  109.0 7.8 %all-to-all-done = bf16[1,2,72,8,128]{4,3,1,0,2:T(8,128)(2,1)S(1)} async-done(((bf16[1,2,72,8,128]{4,3,1,0,2:T(8,128)(2,1)}), bf16[1,2,72,8,128]{4,3,1,0,2:T(8,128)(2,1)S(1)}, u32[]{:S(2)}, u32[]{:S(2)}) %all-to-all-start) | async-done | bytes 294944 | tf_op jit(solution)/shard_map/all_to_all | solution.py:263
  116.9 0.2 abs_reduce_fusion.26
  117.0 0.1 abs_reduce_fusion.25
  117.1 0.1 fusion.5
  117.2 0.7 multiply_subtract_fusion
  (14 shorter events, 0.2 us)
Async XLA Ops:
  2.3 1.5 %collective-permute-start = (bf16[8,88,128]{2,1,0:T(8,128)(2,1)S(1)}, bf16[8,88,128]{2,1,0:T(8,128)(2,1)S(1)}, u32[]{:S(2)}, u32[]{:S(2)}) collective-permute-start(bf16[8,88,128]{2,1,0:T(8,128)(2,1)S(1)} %maximum_bitcast_fusion), channel_id=1, source_target_pairs={{0,2},{2,0},{4,6},{6,4},{8,10},{10,8},{12,14},{14,12},{16,18},{18,... | collective-permute-start | bytes 540680 | tf_op jit(solution)/shard_map/ppermute | solution.py:212
  4.3 4.4 %copy-start.5 = (f32[4,512]{1,0:T(4,128)S(1)}, f32[4,512]{1,0:T(4,128)}, u32[]{:S(2)}) copy-start(f32[4,512]{1,0:T(4,128)} %param.17) | copy-start | bytes 24580
  4.3 4.9 %collective-permute-start.1 = (bf16[4,88,96]{2,1,0:T(8,128)(2,1)S(1)}, bf16[4,88,96]{2,1,0:T(8,128)(2,1)S(1)}, u32[]{:S(2)}, u32[]{:S(2)}) collective-permute-start(bf16[4,88,96]{2,1,0:T(8,128)(2,1)S(1)} %pad_maximum_fusion.2), channel_id=1, source_target_pairs={{0,1},{1,0},{2,3},{3,2},{4,5},{5,4},{6,7},{7,6},{8,9},{9,8},{10,11... | collective-permute-start | bytes 202760 | tf_op jit(solution)/shard_map/ppermute | solution.py:222
  10.0 9.6 %collective-permute-start.2 = (bf16[12,80,128]{2,1,0:T(8,128)(2,1)S(1)}, bf16[12,80,128]{2,1,0:T(8,128)(2,1)S(1)}, u32[]{:S(2)}, u32[]{:S(2)}) collective-permute-start(bf16[12,80,128]{2,1,0:T(8,128)(2,1)S(1)} %get-tuple-element.62), channel_id=1, source_target_pairs={{0,4},{2,6},{4,8},{6,10},{8,12},{10,14},{12,16},{14,18},{16,20},{1... | collective-permute-start | bytes 737288 | tf_op jit(solution)/shard_map/ppermute | solution.py:194
  13.8 5.8 %copy-start.2 = (f32[4,7,512]{2,0,1:T(4,128)S(1)}, f32[4,7,512]{2,0,1:T(4,128)}, u32[]{:S(2)}) copy-start(f32[4,7,512]{2,0,1:T(4,128)} %param.15) | copy-start | bytes 172036
  13.8 5.8 %copy-start.3 = (f32[4,6,512]{2,0,1:T(4,128)S(1)}, f32[4,6,512]{2,0,1:T(4,128)}, u32[]{:S(2)}) copy-start(f32[4,6,512]{2,0,1:T(4,128)} %param.16) | copy-start | bytes 147460
  13.8 5.9 %copy-start.1 = (bf16[512,72]{0,1:T(8,128)(2,1)S(1)}, bf16[512,72]{0,1:T(8,128)(2,1)}, u32[]{:S(2)}) copy-start(bf16[512,72]{0,1:T(8,128)(2,1)} %param.13) | copy-start | bytes 221188
  13.8 5.9 %copy-start.4 = (bf16[512,8]{0,1:T(8,128)(2,1)S(1)}, bf16[512,8]{0,1:T(8,128)(2,1)}, u32[]{:S(2)}) copy-start(bf16[512,8]{0,1:T(8,128)(2,1)} %param.14) | copy-start | bytes 24580
  13.9 9.7 %copy-start = (bf16[72,512]{1,0:T(8,128)(2,1)S(1)}, bf16[72,512]{1,0:T(8,128)(2,1)}, u32[]{:S(2)}) copy-start(bf16[72,512]{1,0:T(8,128)(2,1)} %dec_ref.3) | copy-start | bytes 221188
  13.9 9.6 %collective-permute-start.3 = (bf16[12,80,128]{2,1,0:T(8,128)(2,1)S(1)}, bf16[12,80,128]{2,1,0:T(8,128)(2,1)S(1)}, u32[]{:S(2)}, u32[]{:S(2)}) collective-permute-start(bf16[12,80,128]{2,1,0:T(8,128)(2,1)S(1)} %get-tuple-element.61), channel_id=1, source_target_pairs={{4,0},{6,2},{8,4},{10,6},{12,8},{14,10},{16,12},{18,14},{20,16},{2... | collective-permute-start | bytes 737288 | tf_op jit(solution)/shard_map/ppermute | solution.py:194
  56.6 9.4 %collective-permute-start.4 = (bf16[12,80,128]{2,1,0:T(8,128)(2,1)S(1)}, bf16[12,80,128]{2,1,0:T(8,128)(2,1)S(1)}, u32[]{:S(2)}, u32[]{:S(2)}) collective-permute-start(bf16[12,80,128]{2,1,0:T(8,128)(2,1)S(1)} %get-tuple-element.70), channel_id=1, source_target_pairs={{0,4},{2,6},{4,8},{6,10},{8,12},{10,14},{12,16},{14,18},{16,20},{1... | collective-permute-start | bytes 737288 | tf_op jit(solution)/shard_map/ppermute | solution.py:194
  61.6 9.4 %collective-permute-start.5 = (bf16[12,80,128]{2,1,0:T(8,128)(2,1)S(1)}, bf16[12,80,128]{2,1,0:T(8,128)(2,1)S(1)}, u32[]{:S(2)}, u32[]{:S(2)}) collective-permute-start(bf16[12,80,128]{2,1,0:T(8,128)(2,1)S(1)} %get-tuple-element.69), channel_id=1, source_target_pairs={{4,0},{6,2},{8,4},{10,6},{12,8},{14,10},{16,12},{18,14},{20,16},{2... | collective-permute-start | bytes 737288 | tf_op jit(solution)/shard_map/ppermute | solution.py:194
  98.5 1.7 %collective-permute-start.6 = (bf16[2,8,72,128]{3,2,1,0:T(8,128)(2,1)S(1)}, bf16[2,8,72,128]{3,2,1,0:T(8,128)(2,1)S(1)}, u32[]{:S(2)}, u32[]{:S(2)}) collective-permute-start(bf16[2,8,72,128]{3,2,1,0:T(8,128)(2,1)S(1)} %broadcast_select_fusion.3), channel_id=1, source_target_pairs={{0,2},{2,0},{4,6},{6,4},{8,10},{10,8},{12,14},{14,12},{16,18},{18,... | collective-permute-start | bytes 884744 | tf_op jit(solution)/shard_map/ppermute | solution.py:255
  101.0 15.8 %all-to-all-start = ((bf16[1,2,72,8,128]{4,3,1,0,2:T(8,128)(2,1)}), bf16[1,2,72,8,128]{4,3,1,0,2:T(8,128)(2,1)S(1)}, u32[]{:S(2)}, u32[]{:S(2)}) async-start(bf16[1,2,72,8,128]{4,3,1,0,2:T(8,128)(2,1)} %copy.45), calls=%async_computation | async-start | bytes 589824 | tf_op jit(solution)/shard_map/all_to_all | solution.py:263

commit v4 on v3

--- a/solution.py
+++ b/solution.py
@@ -79,8 +79,8 @@
         tiles = -(-(inset + width - edge - left) // 16)
         out_rows = own + 2 * halo - 2 * edge
 
-        def group(g, _, level=level, edge=edge, tiles=tiles, left=left + 8, deep=4):
-            k = 4 * g
+        def group(g, _, level=level, edge=edge, tiles=tiles, left=left + 8, deep=8):
+            k = 8 * g
 
             def convolve(j, _):
                 c = pl.multiple_of(left + 16 * j, 8)
@@ -146,9 +146,9 @@
                         ] + gate.astype(F32)
             return 0
 
-        lax.fori_loop(0, out_rows // 4, group, 0)
-        if out_rows % 4:
-            group(out_rows // 4, 0, deep=out_rows % 4)
+        lax.fori_loop(0, out_rows // 8, group, 0)
+        if out_rows % 8:
+            group(out_rows // 8, 0, deep=out_rows % 8)
 
     def decode(k, _):
         h = jnp.concatenate([h_ref[t, k, pl.ds(8, span), :] for t in range(planes)], axis=1).astype(BF16)
@@ -169,7 +169,7 @@
     variables = dec.shape[0]
     rows, lanes = own.shape[0], own.shape[2]
     total = rows + 2 * up.shape[0] + 4
-    cells = 64 * (-(-(width - 2 * REACH) // 16))
+    cells = 128 * (-(-(width - 2 * REACH) // 16))
     out_channels = enc.shape[0] if carry_noise else variables
     return pl.pallas_call(
         functools.partial(step_kernel, width),

time: 118 us -> 114 us (0.966)
  Pallas kernels: 60.3 us -> 55.9 us
    pallas_call x2, Pallas kernels: 60.3 us -> 55.9 us  [rollout_step(): pl.pallas_call(functools.partial(step_kernel, width), out_shape=jax.Shape...]
where the time goes in v4:
time: 114 us
  Pallas kernels  55.9 us (49%)
  waiting for transfers between devices  24.8 us (22%)
  starting transfers between devices  21.4 us (19%)
  local copies, waits for them, and re-layouts  6.41 us (6%)
  other arithmetic  4.06 us (4%)
    pallas_call x2, Pallas kernels, rollout_step(): pl.pallas_call(functools.partial(step_kernel, width), out_shape=jax.Shape...  55.9 us
    ppermute x4, waiting for transfers between devices, z_shift(): return lax.ppermute(block, 'lat', pairs)  14 us
    ppermute x4, starting transfers between devices, z_shift(): return lax.ppermute(block, 'lat', pairs)  13.1 us
    all_to_all x1, waiting for transfers between devices, local(): lax.all_to_all(trajectory_predictions, 'member', split_axis=2, concat_axi...  7.8 us
    all_to_all x1, starting transfers between devices, local(): lax.all_to_all(trajectory_predictions, 'member', split_axis=2, concat_axi...  6.51 us
    optimization_barrier x1, local copies, waits for them, and re-layouts, local(): mix, gains, _ = lax.optimization_barrier((mix, gains, packed))  2.79 us
  transfers between devices with their start and end apart: 8, of which 7 were waited for; matrix products, arithmetic and copies ran while one was open for 5% of the time, Pallas kernels for 0%

profile of v4, /device:TPU:32, one launch (start us, length us, event | category | flops | bytes accessed | tf_op | source)
XLA Modules:
  0.0 113.6 jit_solution(7420950689832219429)
XLA Ops:
  0.6 0.7 fusion.18
  1.4 0.9 copy.42
  2.3 0.1 collective-permute-start
  2.5 1.4 %collective-permute-done = bf16[8,88,128]{2,1,0:T(8,128)(2,1)S(1)} collective-permute-done((bf16[8,88,128]{2,1,0:T(8,128)(2,1)S(1)}, bf16[8,88,128]{2,1,0:T(8,128)(2,1)S(1)}, u32[]{:S(2)}, u32[]{:S(2)}) %collective-permute-start) | collective-permute-done | bytes 180256 | tf_op jit(solution)/shard_map/ppermute | solution.py:212
  3.9 0.1 broadcast_select_fusion.4
  3.9 0.2 broadcast_select_fusion.1
  4.1 0.1 pad_maximum_fusion.2
  4.3 0.0 copy-start.5
  4.3 1.6 %collective-permute-start.1 = (bf16[4,88,96]{2,1,0:T(8,128)(2,1)S(1)}, bf16[4,88,96]{2,1,0:T(8,128)(2,1)S(1)}, u32[]{:S(2)}, u32[]{:S(2)}) collective-permute-start(bf16[4,88,96]{2,1,0:T(8,128)(2,1)S(1)} %pad_maximum_fusion.2), channel_id=1, source_target_pairs={{0,1},{1,0},{2,3},{3,2},{4,5},{5,4},{6,7},{7,6},{8,9},{9,8},{10,11... | collective-permute-start | bytes 202760 | tf_op jit(solution)/shard_map/ppermute | solution.py:222
  5.9 2.8 %copy.44 = bf16[4,512,512]{1,2,0:T(8,128)(2,1)S(1)} copy(bf16[4,512,512]{2,1,0:T(8,128)(2,1)} %param.18) | data formatting | bytes 4194304 | tf_op jit(solution)/shard_map/optimization_barrier | solution.py:221
  8.7 0.0 copy-done.5
  8.7 0.5 fusion
  9.2 0.0 collective-permute-done.1
  9.2 0.1 fusion.17
  9.4 0.2 broadcast_select_fusion.2
  9.6 0.3 fusion.12.own_ref
  9.9 0.1 fusion.14
  10.0 3.8 %collective-permute-start.2 = (bf16[12,80,128]{2,1,0:T(8,128)(2,1)S(1)}, bf16[12,80,128]{2,1,0:T(8,128)(2,1)S(1)}, u32[]{:S(2)}, u32[]{:S(2)}) collective-permute-start(bf16[12,80,128]{2,1,0:T(8,128)(2,1)S(1)} %get-tuple-element.62), channel_id=1, source_target_pairs={{0,4},{2,6},{4,8},{6,10},{8,12},{10,14},{12,16},{14,18},{16,20},{1... | collective-permute-start | bytes 737288 | tf_op jit(solution)/shard_map/ppermute | solution.py:194
  13.8 0.0 copy-start.2
  13.8 0.0 copy-start.3
  13.8 0.0 copy-start.1
  13.8 0.0 copy-start.4
  13.9 0.0 copy-start
  13.9 2.2 %collective-permute-start.3 = (bf16[12,80,128]{2,1,0:T(8,128)(2,1)S(1)}, bf16[12,80,128]{2,1,0:T(8,128)(2,1)S(1)}, u32[]{:S(2)}, u32[]{:S(2)}) collective-permute-start(bf16[12,80,128]{2,1,0:T(8,128)(2,1)S(1)} %get-tuple-element.61), channel_id=1, source_target_pairs={{4,0},{6,2},{8,4},{10,6},{12,8},{14,10},{16,12},{18,14},{20,16},{2... | collective-permute-start | bytes 737288 | tf_op jit(solution)/shard_map/ppermute | solution.py:194
  16.0 0.6 fusion.1.mix_ref
  16.6 3.0 %collective-permute-done.2.up_ref = bf16[12,80,128]{2,1,0:T(8,128)(2,1)S(1)} collective-permute-done((bf16[12,80,128]{2,1,0:T(8,128)(2,1)S(1)}, bf16[12,80,128]{2,1,0:T(8,128)(2,1)S(1)}, u32[]{:S(2)}, u32[]{:S(2)}) %collective-permute-start.2) | collective-permute-done | bytes 245792 | tf_op jit(solution)/shard_map/ppermute | solution.py:194
  19.6 0.0 copy-done.2
  19.6 0.0 copy-done.3
  19.7 0.0 copy-done.1
  19.7 0.0 copy-done.4
  19.7 3.8 %collective-permute-done.3.down_ref = bf16[12,80,128]{2,1,0:T(8,128)(2,1)S(1)} collective-permute-done((bf16[12,80,128]{2,1,0:T(8,128)(2,1)S(1)}, bf16[12,80,128]{2,1,0:T(8,128)(2,1)S(1)}, u32[]{:S(2)}, u32[]{:S(2)}) %collective-permute-start.3) | collective-permute-done | bytes 245792 | tf_op jit(solution)/shard_map/ppermute | solution.py:194
  23.5 0.1 broadcast_in_dim.4.taps_ref
  23.6 0.0 copy-done
  23.6 30.6 %rollout_step.2.own_ref = bf16[16,80,128]{2,1,0:T(8,128)(2,1)S(1)} custom-call(bf16[12,80,128]{2,1,0:T(8,128)(2,1)S(1)} %collective-permute-done.2.up_ref, bf16[16,88,128]{2,1,0:T(8,128)(2,1)S(1)} %fusion.12.own_ref, bf16[12,80,128]{2,1,0:T(8,128)(2,1)S(1)} %collective-permute-done.3.down_ref, bf16[80,512]{1,0:T(8,128)(2,1)S(1)} %maximum_bitcast_fusion.1.enc_ref, ...), custom_call_target="tpu_custom_call" | custom-call | tf_op jit(solution)/shard_map/rollout_step/pallas_call | solution.py:174
  54.2 0.1 fusion.16
  54.3 5.0 %collective-permute-start.4 = (bf16[12,80,128]{2,1,0:T(8,128)(2,1)S(1)}, bf16[12,80,128]{2,1,0:T(8,128)(2,1)S(1)}, u32[]{:S(2)}, u32[]{:S(2)}) collective-permute-start(bf16[12,80,128]{2,1,0:T(8,128)(2,1)S(1)} %get-tuple-element.70), channel_id=1, source_target_pairs={{0,4},{2,6},{4,8},{6,10},{8,12},{10,14},{12,16},{14,18},{16,20},{1... | collective-permute-start | bytes 737288 | tf_op jit(solution)/shard_map/ppermute | solution.py:194
  59.3 2.1 %collective-permute-start.5 = (bf16[12,80,128]{2,1,0:T(8,128)(2,1)S(1)}, bf16[12,80,128]{2,1,0:T(8,128)(2,1)S(1)}, u32[]{:S(2)}, u32[]{:S(2)}) collective-permute-start(bf16[12,80,128]{2,1,0:T(8,128)(2,1)S(1)} %get-tuple-element.69), channel_id=1, source_target_pairs={{4,0},{6,2},{8,4},{10,6},{12,8},{14,10},{16,12},{18,14},{20,16},{2... | collective-permute-start | bytes 737288 | tf_op jit(solution)/shard_map/ppermute | solution.py:194
  61.4 2.2 %collective-permute-done.4.up_ref = bf16[12,80,128]{2,1,0:T(8,128)(2,1)S(1)} collective-permute-done((bf16[12,80,128]{2,1,0:T(8,128)(2,1)S(1)}, bf16[12,80,128]{2,1,0:T(8,128)(2,1)S(1)}, u32[]{:S(2)}, u32[]{:S(2)}) %collective-permute-start.4) | collective-permute-done | bytes 245792 | tf_op jit(solution)/shard_map/ppermute | solution.py:194
  63.7 5.0 %collective-permute-done.5.down_ref = bf16[12,80,128]{2,1,0:T(8,128)(2,1)S(1)} collective-permute-done((bf16[12,80,128]{2,1,0:T(8,128)(2,1)S(1)}, bf16[12,80,128]{2,1,0:T(8,128)(2,1)S(1)}, u32[]{:S(2)}, u32[]{:S(2)}) %collective-permute-start.5) | collective-permute-done | bytes 245792 | tf_op jit(solution)/shard_map/ppermute | solution.py:194
  68.7 25.4 %rollout_step.3 = bf16[16,72,128]{2,1,0:T(8,128)(2,1)S(1)} custom-call(bf16[12,80,128]{2,1,0:T(8,128)(2,1)S(1)} %collective-permute-done.4.up_ref, bf16[16,80,128]{2,1,0:T(8,128)(2,1)S(1)} %rollout_step.2.own_ref, bf16[12,80,128]{2,1,0:T(8,128)(2,1)S(1)} %collective-permute-done.5.down_ref, bf16[80,512]{1,0:T(8,128)(2,1)S(1)} %maximum_bitcast_fusion.1.enc_ref, ...), custom_call_target="tpu_custom_call" | custom-call | tf_op jit(solution)/shard_map/rollout_step/pallas_call | solution.py:174
  94.1 0.1 broadcast_select_fusion.3
  94.1 0.1 collective-permute-start.6
  94.2 1.6 %collective-permute-done.6 = bf16[2,8,72,128]{3,2,1,0:T(8,128)(2,1)S(1)} collective-permute-done((bf16[2,8,72,128]{3,2,1,0:T(8,128)(2,1)S(1)}, bf16[2,8,72,128]{3,2,1,0:T(8,128)(2,1)S(1)}, u32[]{:S(2)}, u32[]{:S(2)}) %collective-permute-start.6) | collective-permute-done | bytes 294944 | tf_op jit(solution)/shard_map/ppermute | solution.py:255
  95.8 0.1 select_bitcast_fusion
  95.9 0.7 copy.45
  96.6 6.5 %all-to-all-start = ((bf16[1,2,72,8,128]{4,3,1,0,2:T(8,128)(2,1)}), bf16[1,2,72,8,128]{4,3,1,0,2:T(8,128)(2,1)S(1)}, u32[]{:S(2)}, u32[]{:S(2)}) async-start(bf16[1,2,72,8,128]{4,3,1,0,2:T(8,128)(2,1)} %copy.45), calls=%async_computation | async-start | bytes 589824 | tf_op jit(solution)/shard_map/all_to_all | solution.py:263
  103.1 0.8 dynamic-slice_convert_fusion
  103.9 0.8 copy.47
  104.6 7.8 %all-to-all-done = bf16[1,2,72,8,128]{4,3,1,0,2:T(8,128)(2,1)S(1)} async-done(((bf16[1,2,72,8,128]{4,3,1,0,2:T(8,128)(2,1)}), bf16[1,2,72,8,128]{4,3,1,0,2:T(8,128)(2,1)S(1)}, u32[]{:S(2)}, u32[]{:S(2)}) %all-to-all-start) | async-done | bytes 294944 | tf_op jit(solution)/shard_map/all_to_all | solution.py:263
  112.5 0.2 abs_reduce_fusion.26
  112.7 0.1 abs_reduce_fusion.25
  112.7 0.1 fusion.5
  112.8 0.7 multiply_subtract_fusion
  (14 shorter events, 0.2 us)
Async XLA Ops:
  2.3 1.5 %collective-permute-start = (bf16[8,88,128]{2,1,0:T(8,128)(2,1)S(1)}, bf16[8,88,128]{2,1,0:T(8,128)(2,1)S(1)}, u32[]{:S(2)}, u32[]{:S(2)}) collective-permute-start(bf16[8,88,128]{2,1,0:T(8,128)(2,1)S(1)} %maximum_bitcast_fusion), channel_id=1, source_target_pairs={{0,2},{2,0},{4,6},{6,4},{8,10},{10,8},{12,14},{14,12},{16,18},{18,... | collective-permute-start | bytes 540680 | tf_op jit(solution)/shard_map/ppermute | solution.py:212
  4.3 4.4 %copy-start.5 = (f32[4,512]{1,0:T(4,128)S(1)}, f32[4,512]{1,0:T(4,128)}, u32[]{:S(2)}) copy-start(f32[4,512]{1,0:T(4,128)} %param.17) | copy-start | bytes 24580
  4.3 4.9 %collective-permute-start.1 = (bf16[4,88,96]{2,1,0:T(8,128)(2,1)S(1)}, bf16[4,88,96]{2,1,0:T(8,128)(2,1)S(1)}, u32[]{:S(2)}, u32[]{:S(2)}) collective-permute-start(bf16[4,88,96]{2,1,0:T(8,128)(2,1)S(1)} %pad_maximum_fusion.2), channel_id=1, source_target_pairs={{0,1},{1,0},{2,3},{3,2},{4,5},{5,4},{6,7},{7,6},{8,9},{9,8},{10,11... | collective-permute-start | bytes 202760 | tf_op jit(solution)/shard_map/ppermute | solution.py:222
  10.0 9.6 %collective-permute-start.2 = (bf16[12,80,128]{2,1,0:T(8,128)(2,1)S(1)}, bf16[12,80,128]{2,1,0:T(8,128)(2,1)S(1)}, u32[]{:S(2)}, u32[]{:S(2)}) collective-permute-start(bf16[12,80,128]{2,1,0:T(8,128)(2,1)S(1)} %get-tuple-element.62), channel_id=1, source_target_pairs={{0,4},{2,6},{4,8},{6,10},{8,12},{10,14},{12,16},{14,18},{16,20},{1... | collective-permute-start | bytes 737288 | tf_op jit(solution)/shard_map/ppermute | solution.py:194
  13.8 5.8 %copy-start.2 = (f32[4,7,512]{2,0,1:T(4,128)S(1)}, f32[4,7,512]{2,0,1:T(4,128)}, u32[]{:S(2)}) copy-start(f32[4,7,512]{2,0,1:T(4,128)} %param.15) | copy-start | bytes 172036
  13.8 5.8 %copy-start.3 = (f32[4,6,512]{2,0,1:T(4,128)S(1)}, f32[4,6,512]{2,0,1:T(4,128)}, u32[]{:S(2)}) copy-start(f32[4,6,512]{2,0,1:T(4,128)} %param.16) | copy-start | bytes 147460
  13.8 5.9 %copy-start.1 = (bf16[512,72]{0,1:T(8,128)(2,1)S(1)}, bf16[512,72]{0,1:T(8,128)(2,1)}, u32[]{:S(2)}) copy-start(bf16[512,72]{0,1:T(8,128)(2,1)} %param.13) | copy-start | bytes 221188
  13.8 5.9 %copy-start.4 = (bf16[512,8]{0,1:T(8,128)(2,1)S(1)}, bf16[512,8]{0,1:T(8,128)(2,1)}, u32[]{:S(2)}) copy-start(bf16[512,8]{0,1:T(8,128)(2,1)} %param.14) | copy-start | bytes 24580
  13.9 9.7 %copy-start = (bf16[72,512]{1,0:T(8,128)(2,1)S(1)}, bf16[72,512]{1,0:T(8,128)(2,1)}, u32[]{:S(2)}) copy-start(bf16[72,512]{1,0:T(8,128)(2,1)} %dec_ref.3) | copy-start | bytes 221188
  13.9 9.6 %collective-permute-start.3 = (bf16[12,80,128]{2,1,0:T(8,128)(2,1)S(1)}, bf16[12,80,128]{2,1,0:T(8,128)(2,1)S(1)}, u32[]{:S(2)}, u32[]{:S(2)}) collective-permute-start(bf16[12,80,128]{2,1,0:T(8,128)(2,1)S(1)} %get-tuple-element.61), channel_id=1, source_target_pairs={{4,0},{6,2},{8,4},{10,6},{12,8},{14,10},{16,12},{18,14},{20,16},{2... | collective-permute-start | bytes 737288 | tf_op jit(solution)/shard_map/ppermute | solution.py:194
  54.3 9.4 %collective-permute-start.4 = (bf16[12,80,128]{2,1,0:T(8,128)(2,1)S(1)}, bf16[12,80,128]{2,1,0:T(8,128)(2,1)S(1)}, u32[]{:S(2)}, u32[]{:S(2)}) collective-permute-start(bf16[12,80,128]{2,1,0:T(8,128)(2,1)S(1)} %get-tuple-element.70), channel_id=1, source_target_pairs={{0,4},{2,6},{4,8},{6,10},{8,12},{10,14},{12,16},{14,18},{16,20},{1... | collective-permute-start | bytes 737288 | tf_op jit(solution)/shard_map/ppermute | solution.py:194
  59.3 9.4 %collective-permute-start.5 = (bf16[12,80,128]{2,1,0:T(8,128)(2,1)S(1)}, bf16[12,80,128]{2,1,0:T(8,128)(2,1)S(1)}, u32[]{:S(2)}, u32[]{:S(2)}) collective-permute-start(bf16[12,80,128]{2,1,0:T(8,128)(2,1)S(1)} %get-tuple-element.69), channel_id=1, source_target_pairs={{4,0},{6,2},{8,4},{10,6},{12,8},{14,10},{16,12},{18,14},{20,16},{2... | collective-permute-start | bytes 737288 | tf_op jit(solution)/shard_map/ppermute | solution.py:194
  94.1 1.7 %collective-permute-start.6 = (bf16[2,8,72,128]{3,2,1,0:T(8,128)(2,1)S(1)}, bf16[2,8,72,128]{3,2,1,0:T(8,128)(2,1)S(1)}, u32[]{:S(2)}, u32[]{:S(2)}) collective-permute-start(bf16[2,8,72,128]{3,2,1,0:T(8,128)(2,1)S(1)} %broadcast_select_fusion.3), channel_id=1, source_target_pairs={{0,2},{2,0},{4,6},{6,4},{8,10},{10,8},{12,14},{14,12},{16,18},{18,... | collective-permute-start | bytes 884744 | tf_op jit(solution)/shard_map/ppermute | solution.py:255
  96.6 15.8 %all-to-all-start = ((bf16[1,2,72,8,128]{4,3,1,0,2:T(8,128)(2,1)}), bf16[1,2,72,8,128]{4,3,1,0,2:T(8,128)(2,1)S(1)}, u32[]{:S(2)}, u32[]{:S(2)}) async-start(bf16[1,2,72,8,128]{4,3,1,0,2:T(8,128)(2,1)} %copy.45), calls=%async_computation | async-start | bytes 589824 | tf_op jit(solution)/shard_map/all_to_all | solution.py:263
